TPU v7x, 512 devices: a whole 4x4x16 slice. The times are simulated.
512 devices in a mesh: cols: 16 (over y_lo, x, core), trc: 16 (over z), lev: 2 (over y_hi).
Axes of the slice: x: 4, y: 4 (y_hi: 2, y_lo: 2; y = y_hi * 2 + y_lo), z: 16, core: 2. Of those that a mesh axis runs over, the one named last changes fastest.
Arguments:
- potential_warmth: float32 [128, 128, 128], P('lev', 'cols', 'trc'), may hold values from -6 to 6
- saltiness_anomaly: float32 [128, 128, 128], P('lev', 'cols', 'trc'), may hold values from -6 to 6
- zonal_speed: float32 [128, 128, 128], P('lev', 'cols', 'trc'), may hold values from -3 to 3
- meridional_speed: float32 [128, 128, 128], P('lev', 'cols', 'trc'), may hold values from -3 to 3
- marine_indicator: int32 [128, 128, 128], P('lev', 'cols', 'trc'), may hold values from 0 to 1, as said below
- species_concentrations: float32 [64, 128, 128, 128], P('trc', 'lev', 'cols'), may hold values from 0.1 to 2
- coupling_matrix: bfloat16 [64, 64], replicated, may hold values from -0.75 to 0.75
- species_guild_number: int32 [64], replicated, may hold values from 0 to 7
- guild_extinction_coefficient: float32 [8], replicated, may hold values from 0.0001 to 0.0012
Outputs:
- warmth_final: float32 [128, 128, 128], P('lev', 'cols', 'trc')
- saltiness_final: float32 [128, 128, 128], P('lev', 'cols', 'trc')
- zonal_speed_final: float32 [128, 128, 128], P('lev', 'cols', 'trc')
- meridional_speed_final: float32 [128, 128, 128], P('lev', 'cols', 'trc')
- species_final: float32 [64, 128, 128, 128], P('trc', 'lev', 'cols')
Inputs may be any that keep to these rules, and one draw needn't show every extreme that they name: `marine_indicator`: each column is sea from level 0 down to a depth drawn per column and land below it; the columns at the first index and at the last two indices of the second horizontal dimension are sea at every level.
All inputs are finite; a program needn't handle non-finite values.
Results may differ from a plain program's by a relative error of at most 0.00066.
Values may be sent and summed in bfloat16 or wider, within the bound.
A program may use at most 64 MiB of HBM per device.

v0:
```python
import jax
import jax.numpy as jnp
from jax import lax
from jax.sharding import PartitionSpec as P

viscosity = 0.2
buoyancy = 0.25
marine_advance = 0.05
tracer_step = 0.2
level_step = 0.04
react_step = 0.25
warming_amount = 60.0


def entering(part, axis, combine, identity, reverse):
    count = lax.axis_size(axis)
    place = lax.axis_index(axis)
    ahead = count - 1 - place if reverse else place
    gathered = lax.all_gather(part, axis)
    state = jnp.zeros_like(part) + jnp.asarray(identity, part.dtype)

    def one(turn, state):
        source = count - 1 - turn if reverse else turn
        return combine(state, lax.dynamic_index_in_dim(gathered, source, 0, False))

    return lax.fori_loop(0, ahead, one, state)


def extended(block, sides, width, periodic):
    for axis, dim in sides:
        count = lax.axis_size(axis)
        forward = [(i, i + 1) for i in range(count - 1)]
        if periodic:
            forward.append((count - 1, 0))
        backward = [(target, source) for source, target in forward]
        low = lax.ppermute(
            lax.slice_in_dim(block, block.shape[dim] - width, None, axis=dim), axis, forward
        )
        high = lax.ppermute(lax.slice_in_dim(block, 0, width, axis=dim), axis, backward)
        block = jnp.concatenate([low, block, high], axis=dim)
    return block


def from_behind(value, axis, steps):
    count = lax.axis_size(axis)
    pairs = [(source, (source + steps) % count) for source in range(count)]
    return lax.ppermute(value, axis, pairs)


def minmod(slope_left, slope_right):
    return (
        0.5
        * (jnp.sign(slope_left) + jnp.sign(slope_right))
        * jnp.minimum(jnp.abs(slope_left), jnp.abs(slope_right))
    )


def limited_div(padded, face_speed, dimension):
    length = padded.shape[dimension] - 4
    far_left = lax.slice_in_dim(padded, 0, length + 1, axis=dimension)
    left_cell = lax.slice_in_dim(padded, 1, length + 2, axis=dimension)
    right_cell = lax.slice_in_dim(padded, 2, length + 3, axis=dimension)
    far_right = lax.slice_in_dim(padded, 3, length + 4, axis=dimension)
    plus_side = left_cell + 0.5 * minmod(left_cell - far_left, right_cell - left_cell)
    minus_side = right_cell - 0.5 * minmod(right_cell - left_cell, far_right - right_cell)
    face_flux = jnp.maximum(face_speed, 0.0) * plus_side + jnp.minimum(face_speed, 0.0) * minus_side
    return lax.slice_in_dim(face_flux, 1, length + 1, axis=dimension) - lax.slice_in_dim(
        face_flux, 0, length, axis=dimension
    )


def add_up(earlier, latter):
    return earlier + latter


def shards(
    potential_warmth,
    saltiness_anomaly,
    zonal_speed,
    meridional_speed,
    marine_indicator,
    species_concentrations,
    coupling_matrix,
    species_guild_number,
    guild_extinction_coefficient,
):
    layer_sum = potential_warmth.shape[0]
    marine_indicator_real = marine_indicator.astype(jnp.float32)
    fluid_mass_per_volume = 0.8 * saltiness_anomaly - 0.2 * potential_warmth
    profile_beginning = jnp.zeros(potential_warmth.shape[1:], jnp.float32)
    above_density = entering(
        jnp.sum(fluid_mass_per_volume, axis=0), "lev", add_up, profile_beginning, False
    )
    hydrostatic_pressure = buoyancy * (
        above_density[None]
        + jnp.cumsum(fluid_mass_per_volume, axis=0)
        - 0.5 * fluid_mass_per_volume
    )
    stacked_fields = jnp.stack(
        [
            hydrostatic_pressure,
            zonal_speed,
            meridional_speed,
            marine_indicator_real,
            potential_warmth,
            saltiness_anomaly,
        ]
    )
    padded_block = extended(stacked_fields, (("cols", 2), ("trc", 3), ("lev", 1)), 1, True)
    east_side = padded_block[:, 1:-1, 2:, 1:-1]
    west_side = padded_block[:, 1:-1, :-2, 1:-1]
    north_side = padded_block[:, 1:-1, 1:-1, 2:]
    south_side = padded_block[:, 1:-1, 1:-1, :-2]
    mask_east = marine_indicator_real * east_side[3]
    mask_north = marine_indicator_real * north_side[3]
    east_laplace = east_side[1] + west_side[1] + north_side[1] + south_side[1] - 4.0 * zonal_speed
    north_laplace = (
        east_side[2] + west_side[2] + north_side[2] + south_side[2] - 4.0 * meridional_speed
    )
    zonal_speed_final = mask_east * (
        zonal_speed
        + marine_advance * (-(east_side[0] - hydrostatic_pressure) + viscosity * east_laplace)
    )
    meridional_speed_final = mask_north * (
        meridional_speed
        + marine_advance * (-(north_side[0] - hydrostatic_pressure) + viscosity * north_laplace)
    )
    east_west = from_behind(zonal_speed_final[:, -1:, :], "cols", 1)
    north_south = from_behind(meridional_speed_final[:, :, -1:], "trc", 1)
    faces_east = jnp.concatenate([east_west, zonal_speed_final], axis=1)
    faces_north = jnp.concatenate([north_south, meridional_speed_final], axis=2)
    divergence = (
        zonal_speed_final - faces_east[:, :-1] + meridional_speed_final - faces_north[:, :, :-1]
    )
    flow_next = entering(jnp.sum(divergence, axis=0), "lev", add_up, profile_beginning, True)
    deeper_sum = jnp.cumsum(divergence[::-1], axis=0)[::-1] + flow_next[None]
    level_index = lax.axis_index("lev") * layer_sum + lax.broadcasted_iota(
        jnp.int32, deeper_sum.shape, 0
    )
    faces_vertical = jnp.concatenate(
        [jnp.where(level_index == 0, 0.0, deeper_sum), flow_next[None]], axis=0
    )

    def donor_quantity(member):
        values = padded_block[member]
        cells_east = values[1:-1, :, 1:-1]
        flux_east = (
            jnp.maximum(faces_east, 0.0) * cells_east[:, :-1]
            + jnp.minimum(faces_east, 0.0) * cells_east[:, 1:]
        )
        cells_north = values[1:-1, 1:-1, :]
        flux_north = (
            jnp.maximum(faces_north, 0.0) * cells_north[:, :, :-1]
            + jnp.minimum(faces_north, 0.0) * cells_north[:, :, 1:]
        )
        cells_down = values[:, 1:-1, 1:-1]
        flux_down = (
            jnp.maximum(faces_vertical, 0.0) * cells_down[:-1]
            + jnp.minimum(faces_vertical, 0.0) * cells_down[1:]
        )
        return (
            flux_east[:, 1:]
            - flux_east[:, :-1]
            + (flux_north[:, :, 1:] - flux_north[:, :, :-1])
            + (flux_down[1:] - flux_down[:-1])
        )

    tracer_east, tracer_north, tracer_down = (
        lax.all_gather(faces_east, "trc", axis=2, tiled=True),
        lax.all_gather(meridional_speed_final, "trc", axis=2, tiled=True),
        lax.all_gather(faces_vertical, "trc", axis=2, tiled=True),
    )
    tracer_faces_north = jnp.concatenate([tracer_north[:, :, -1:], tracer_north], axis=2)
    advected = species_concentrations
    for repeat in range(2):
        beside = extended(advected, (("cols", 2),), 2, True)
        stacks = extended(advected, (("lev", 1),), 2, False)
        beside_all = jnp.concatenate([advected[..., -2:], advected, advected[..., :2]], axis=3)
        sideways = limited_div(beside, tracer_east[None], 2) + limited_div(
            beside_all, tracer_faces_north[None], 3
        )
        upright = limited_div(stacks, tracer_down[None], 1)
        advected = advected - (tracer_step * sideways + level_step * upright)
    rounded = lax.optimization_barrier(advected.astype(jnp.bfloat16))
    onehot = (
        species_guild_number[:, None]
        == lax.broadcasted_iota(
            jnp.int32, (species_guild_number.shape[0], guild_extinction_coefficient.shape[0]), 1
        )
    ).astype(jnp.float32)
    absorb = jnp.sum(onehot * guild_extinction_coefficient[None, :], axis=1)
    group_size = species_concentrations.shape[0]
    own_start = lax.axis_index("trc") * group_size
    own_rows = lax.dynamic_slice_in_dim(coupling_matrix, own_start, group_size, 0)
    reaction = jnp.einsum(
        "st,tzxy->szxy",
        own_rows,
        lax.all_gather(rounded, "trc", axis=0, tiled=True),
        preferred_element_type=jnp.float32,
    )
    own_absorb = lax.dynamic_slice_in_dim(absorb, own_start, group_size, 0)
    partial_sum = jnp.sum(own_absorb[:, None, None, None] * rounded.astype(jnp.float32), axis=0)
    attenuation = lax.psum_scatter(partial_sum, "trc", scatter_dimension=2, tiled=True)
    species_final = advected + react_step * reaction
    light_top = entering(jnp.sum(attenuation, axis=0), "lev", add_up, profile_beginning, False)
    light_path = light_top[None] + jnp.cumsum(attenuation, axis=0) - attenuation
    radiation_captured = jnp.exp(-light_path) * (1.0 - jnp.exp(-attenuation))
    warmth_final = (
        potential_warmth
        - marine_advance * donor_quantity(4)
        + warming_amount * marine_indicator_real * radiation_captured
    )
    saltiness_final = saltiness_anomaly - marine_advance * donor_quantity(5)
    return (warmth_final, saltiness_final, zonal_speed_final, meridional_speed_final, species_final)


def solution(mesh):
    in_specs = (
        P("lev", "cols", "trc"),
        P("lev", "cols", "trc"),
        P("lev", "cols", "trc"),
        P("lev", "cols", "trc"),
        P("lev", "cols", "trc"),
        P("trc", "lev", "cols", None),
        P(),
        P(),
        P(),
    )
    out_specs = (
        P("lev", "cols", "trc"),
        P("lev", "cols", "trc"),
        P("lev", "cols", "trc"),
        P("lev", "cols", "trc"),
        P("trc", "lev", "cols", None),
    )
    return jax.shard_map(shards, mesh=mesh, in_specs=in_specs, out_specs=out_specs, check_vma=False)
```

profile of v0, /device:TPU:1, one launch (start us, length us, event | category | flops | bytes accessed | tf_op | source)
XLA Modules:
  0.0 446.1 jit_solution(10437617223934750346)
XLA Ops:
  8.4 6.3 %fusion.94 = f32[64,8,8]{2,1,0:T(8,128)S(1)} fusion(f32[64,8,8]{2,1,0:T(8,128)S(1)} %copy.303), kind=kOutput, calls=%fused_computation.202 | output fusion | flops 258048 | bytes 32768 | tf_op jit(solution)/shard_map/jit(cumsum)/reduce_window_sum | solution.py:96
  14.9 5.5 %all-gather = f32[16,8]{1,0:T(8,128)S(1)} all-gather(f32[8,8]{1,0:T(8,128)S(1)} %get-tuple-element.227), channel_id=2, replica_groups=mesh['cols'=16,'trc'=16,'lev'=2] {'lev'}, dimensions={0}, use_global_device_ids=true | all-gather | bytes 768 | tf_op jit(solution)/shard_map/all_gather | solution.py:19
  20.5 9.1 %collective-permute-start = (f32[6,64,1,8]{1,3,2,0:T(8,128)S(1)}, f32[6,64,1,8]{1,3,2,0:T(8,128)S(1)}, u32[]{:S(2)}, u32[]{:S(2)}) collective-permute-start(f32[6,64,1,8]{1,3,2,0:T(8,128)S(1)} %get-tuple-element.258), channel_id=1, source_target_pairs={{32,0},{64,32},{96,64},{128,96},{160,128},{192,160},{224,192},{256... | collective-permute-start | bytes 36872 | tf_op jit(solution)/shard_map/ppermute | solution.py:39
  29.7 1.9 collective-permute-start.1
  35.7 2.2 collective-permute-start.10
  39.4 1.9 fusion.89
  41.5 3.0 collective-permute-start.3
  44.5 9.5 %collective-permute-start.2 = (f32[6,64,10,1]{1,3,2,0:T(1,128)S(1)}, f32[6,64,10,1]{1,3,2,0:T(1,128)S(1)}, u32[]{:S(2)}, u32[]{:S(2)}) collective-permute-start(f32[6,64,10,1]{1,3,2,0:T(1,128)S(1)} %get-tuple-element.255), channel_id=1, source_target_pairs={{2,0},{4,2},{6,4},{8,6},{10,8},{12,10},{14,12},{16,14},{18,16},{20... | collective-permute-start | bytes 46088 | tf_op jit(solution)/shard_map/ppermute | solution.py:39
  55.9 24.9 %all_gather.35 = f32[64,8,128]{0,1,2:T(8,128)S(1)} all-gather(f32[64,8,8]{0,1,2:T(8,128)S(1)} %copy.326), channel_id=1, replica_groups=mesh['cols'=16,'trc'=16,'lev'=2] {'trc'}, dimensions={2}, use_global_device_ids=true | all-gather | bytes 278528 | tf_op jit(solution)/shard_map/all_gather | solution.py:170
  85.2 11.4 %collective-permute-start.4 = (f32[64,1,8]{0,2,1:T(8,128)S(1)}, f32[64,1,8]{0,2,1:T(8,128)S(1)}, u32[]{:S(2)}, u32[]{:S(2)}) collective-permute-start(f32[64,1,8]{0,2,1:T(8,128)S(1)} %slice.454), channel_id=1, source_target_pairs={{0,32},{32,64},{64,96},{96,128},{128,160},{160,192},{192,224},{224... | collective-permute-start | bytes 6152 | tf_op jit(solution)/shard_map/ppermute | solution.py:47
  98.6 9.9 %multiply_add_fusion.1 = f32[4,64,8,129]{3,0,2,1:T(4,128)} fusion(f32[4,64,8,2]{3,0,2,1:T(4,128)} %get-tuple-element.244, f32[4,64,8,128]{3,0,2,1:T(4,128)S(1)} %copy.340, f32[4,64,8,2]{3,0,2,1:T(4,128)} %get-tuple-element.243, f32[64,8,129]{2,1,0:T(8,128)S(1)} %get-tuple-element.248, f32[64,8,129]{2,1,0:T(8,128)S(1)} %get-tuple-element.247), kind=kLoop, calls=%fused_computation.18 | loop fusion | flops 7397376 | bytes 2666496 | tf_op jit(solution)/shard_map/add | solution.py:66
  109.1 2.0 fusion.91
  111.1 6.4 %collective-permute-start.6 = (f32[6,1,10,10]{1,0,3,2:T(8,128)}, f32[6,1,10,10]{1,0,3,2:T(8,128)}, u32[]{:S(2)}, u32[]{:S(2)}) collective-permute-start(f32[6,1,10,10]{1,0,3,2:T(8,128)} %get-tuple-element.250), channel_id=1, source_target_pairs={{1,0},{0,1},{3,2},{2,3},{5,4},{4,5},{7,6},{6,7},{9,8},{8,9},{11,10... | collective-permute-start | bytes 7208 | tf_op jit(solution)/shard_map/ppermute | solution.py:39
  117.5 1.9 collective-permute-start.5
  119.5 16.0 %all-gather.1 = f32[16,8]{1,0:T(8,128)S(1)} all-gather(f32[8,8]{1,0:T(8,128)S(1)} %get-tuple-element.223), channel_id=3, replica_groups=mesh['cols'=16,'trc'=16,'lev'=2] {'lev'}, dimensions={0}, use_global_device_ids=true | all-gather | bytes 768 | tf_op jit(solution)/shard_map/all_gather | solution.py:19
  135.8 6.3 %fusion.95 = f32[64,8,8]{2,1,0:T(8,128)S(1)} fusion(f32[64,8,8]{2,1,0:T(8,128)S(1)} %copy.312), kind=kOutput, calls=%fused_computation.203 | output fusion | flops 258048 | bytes 32768 | tf_op jit(solution)/shard_map/jit(cumsum)/reduce_window_sum | solution.py:136
  144.5 2.1 pad_maximum_fusion.11
  148.0 25.7 %all_gather.36 = f32[65,8,128]{0,1,2:T(8,128)S(1)} all-gather(f32[65,8,8]{0,1,2:T(8,128)S(1)} %copy.333), channel_id=1, replica_groups=mesh['cols'=16,'trc'=16,'lev'=2] {'trc'}, dimensions={2}, use_global_device_ids=true | all-gather | bytes 282880 | tf_op jit(solution)/shard_map/all_gather | solution.py:171
  174.7 23.1 %all_gather.34 = f32[64,9,128]{0,2,1:T(8,128)S(1)} all-gather(f32[64,9,8]{0,2,1:T(8,128)S(1)} %get-tuple-element.261), channel_id=1, replica_groups=mesh['cols'=16,'trc'=16,'lev'=2] {'trc'}, dimensions={2}, use_global_device_ids=true | all-gather | bytes 313344 | tf_op jit(solution)/shard_map/all_gather | solution.py:169
  202.3 2.9 multiply_add_fusion.5
  206.2 3.3 multiply_add_fusion.3
  213.1 5.5 %collective-permute-start.14 = (f32[4,2,8,128]{3,0,2,1:T(4,128)S(1)}, f32[4,2,8,128]{3,0,2,1:T(4,128)S(1)}, u32[]{:S(2)}, u32[]{:S(2)}) collective-permute-start(f32[4,2,8,128]{3,0,2,1:T(4,128)S(1)} %get-tuple-element.235), channel_id=1, source_target_pairs={{0,1},{2,3},{4,5},{6,7},{8,9},{10,11},{12,13},{14,15},{16,17},{18,... | collective-permute-start | bytes 98312 | tf_op jit(solution)/shard_map/ppermute | solution.py:36
  218.6 18.1 %collective-permute-start.13 = (f32[4,64,2,128]{3,0,2,1:T(4,128)S(1)}, f32[4,64,2,128]{3,0,2,1:T(4,128)S(1)}, u32[]{:S(2)}, u32[]{:S(2)}) collective-permute-start(f32[4,64,2,128]{3,0,2,1:T(4,128)S(1)} %get-tuple-element.232), channel_id=1, source_target_pairs={{32,0},{64,32},{96,64},{128,96},{160,128},{192,160},{224,192},{256... | collective-permute-start | bytes 786440 | tf_op jit(solution)/shard_map/ppermute | solution.py:39
  236.8 2.1 collective-permute-start.12
  238.9 7.6 %multiply_add_fusion = f32[4,64,8,129]{3,0,2,1:T(4,128)S(1)} fusion(f32[4,64,8,2]{3,0,2,1:T(4,128)S(1)} %get-tuple-element.234, f32[4,64,8,128]{3,0,2,1:T(4,128)S(1)} %fusion.27, f32[4,64,8,2]{3,0,2,1:T(4,128)S(1)} %get-tuple-element.233, f32[64,8,129]{2,1,0:T(8,128)S(1)} %get-tuple-element.248, f32[64,8,129]{2,1,0:T(8,128)S(1)} %get-tuple-element.247), kind=kLoop, calls=%fused_computation.17 | loop fusion | flops 7397376 | bytes 2666496 | tf_op jit(solution)/shard_map/add | solution.py:66
  246.6 3.2 multiply_add_fusion.4
  249.8 4.5 %multiply_add_fusion.2 = f32[4,64,9,128]{3,0,2,1:T(4,128)S(1)} fusion(f32[4,64,2,128]{3,0,2,1:T(4,128)S(1)} %collective-permute-done.13, f32[4,64,8,128]{3,0,2,1:T(4,128)S(1)} %fusion.27, f32[4,64,2,128]{3,0,2,1:T(4,128)S(1)} %collective-permute-done.12, f32[64,9,128]{2,1,0:T(8,128)S(1)} %copy.325, f32[64,9,128]{2,1,0:T(8,128)S(1)} %copy.319), kind=kLoop, calls=%fused_computation.33 | loop fusion | flops 8257536 | bytes 3342336 | tf_op jit(solution)/shard_map/add | solution.py:66
  259.2 54.5 %reduce-scatter.2.cloned.1.call-done = f32[64,8,8]{0,1,2:T(8,128)} async-done(((f32[64,8,128]{0,1,2:T(8,128)}), f32[64,8,8]{0,1,2:T(8,128)}) %reduce-scatter.2.cloned.1.call-update) | async-done | bytes 16400 | tf_op jit(solution)/shard_map/reduce_scatter | solution.py:203
  314.7 6.3 %fusion.96 = f32[64,8,8]{2,1,0:T(8,128)S(1)} fusion(f32[64,8,8]{2,1,0:T(8,128)S(1)} %copy.342), kind=kOutput, calls=%fused_computation.204 | output fusion | flops 258048 | bytes 32768 | tf_op jit(solution)/shard_map/jit(cumsum)/reduce_window_sum | solution.py:206
  322.1 4.7 %all-gather.2 = f32[16,8]{1,0:T(8,128)S(1)} all-gather(f32[8,8]{1,0:T(8,128)S(1)} %copy.359), channel_id=4, replica_groups=mesh['cols'=16,'trc'=16,'lev'=2] {'lev'}, dimensions={0}, use_global_device_ids=true | all-gather | bytes 768 | tf_op jit(solution)/shard_map/all_gather | solution.py:19
  327.8 102.3 %all-gather.5.cloned.1.call-done = bf16[64,64,8,128]{3,2,1,0:T(8,128)(2,1)} async-done(((bf16[4,64,8,128]{3,2,1,0:T(8,128)(2,1)}), bf16[64,64,8,128]{3,2,1,0:T(8,128)(2,1)}) %all-gather.5.cloned.1.call-update) | async-done | bytes 8388624 | tf_op jit(solution)/shard_map/all_gather | solution.py:198
  430.1 8.1 %fusion.9 = f32[4,64,8,128]{3,0,2,1:T(4,128)S(1)} fusion(f32[4,64,8,128]{3,0,2,1:T(4,128)S(1)} %get-tuple-element.222, bf16[64,64,8,128]{3,2,1,0:T(8,128)(2,1)} %all-gather.5.cloned.1.call-done, bf16[64,64]{1,0:T(8,128)(2,1)S(1)} %copy-done, s32[]{:T(128)S(6)} %select_n.23), kind=kOutput, calls=%fused_computation.24 | convolution fusion | flops 34078720 | bytes 10486788 | tf_op jit(solution)/shard_map/st,tzxy->szxy/dot_general | solution.py:195
  (153 shorter events, 38.8 us)
Async XLA Ops:
  7.2 423.0 %copy-start = (bf16[64,64]{1,0:T(8,128)(2,1)S(1)}, bf16[64,64]{1,0:T(8,128)(2,1)}, u32[]{:S(2)}) copy-start(bf16[64,64]{1,0:T(8,128)(2,1)} %param.21) | copy-start | bytes 24580
  7.2 13.3 %copy-start.6 = (f32[64,8,8]{0,2,1:T(8,128)S(1)}, f32[64,8,8]{0,2,1:T(8,128)}, u32[]{:S(2)}) copy-start(f32[64,8,8]{0,2,1:T(8,128)} %param.15) | copy-start | bytes 49156
  7.2 13.3 %copy-start.9 = (f32[64,8,8]{0,2,1:T(8,128)S(1)}, f32[64,8,8]{0,2,1:T(8,128)}, u32[]{:S(2)}) copy-start(f32[64,8,8]{0,2,1:T(8,128)} %param.16) | copy-start | bytes 49156
  7.2 13.2 %copy-start.4 = (s32[64,8,8]{0,2,1:T(8,128)S(1)}, s32[64,8,8]{0,2,1:T(8,128)}, u32[]{:S(2)}) copy-start(s32[64,8,8]{0,2,1:T(8,128)} %param.19) | copy-start | bytes 49156
  7.2 24.4 %copy-start.1 = (f32[4,64,8,128]{3,2,1,0:T(8,128)S(1)}, f32[4,64,8,128]{3,2,1,0:T(8,128)}, u32[]{:S(2)}) copy-start(f32[4,64,8,128]{3,2,1,0:T(8,128)} %param.20) | copy-start | bytes 3145732
  7.2 306.5 %reduce-scatter.2.cloned.1.call-start = ((), (), s32[]{:S(2)}) async-start(), calls=%async_computation.1 | async-start | bytes 557056 | tf_op jit(solution)/shard_map/reduce_scatter | solution.py:203
  20.5 20.9 %collective-permute-start = (f32[6,64,1,8]{1,3,2,0:T(8,128)S(1)}, f32[6,64,1,8]{1,3,2,0:T(8,128)S(1)}, u32[]{:S(2)}, u32[]{:S(2)}) collective-permute-start(f32[6,64,1,8]{1,3,2,0:T(8,128)S(1)} %get-tuple-element.258), channel_id=1, source_target_pairs={{32,0},{64,32},{96,64},{128,96},{160,128},{192,160},{224,192},{256... | collective-permute-start | bytes 36872 | tf_op jit(solution)/shard_map/ppermute | solution.py:39
  29.7 11.7 %collective-permute-start.1 = (f32[6,64,1,8]{1,3,2,0:T(8,128)S(1)}, f32[6,64,1,8]{1,3,2,0:T(8,128)S(1)}, u32[]{:S(2)}, u32[]{:S(2)}) collective-permute-start(f32[6,64,1,8]{1,3,2,0:T(8,128)S(1)} %get-tuple-element.257), channel_id=1, source_target_pairs={{0,32},{32,64},{64,96},{96,128},{128,160},{160,192},{192,224},{224... | collective-permute-start | bytes 36872 | tf_op jit(solution)/shard_map/ppermute | solution.py:36
  33.2 166.1 %collective-permute-start.8 = (f32[4,64,2,128]{3,0,2,1:T(4,128)}, f32[4,64,2,128]{3,0,2,1:T(4,128)}, u32[]{:S(2)}, u32[]{:S(2)}) collective-permute-start(f32[4,64,2,128]{3,0,2,1:T(4,128)} %get-tuple-element.241), channel_id=1, source_target_pairs={{0,32},{32,64},{64,96},{96,128},{128,160},{160,192},{192,224},{224... | collective-permute-start | bytes 786440 | tf_op jit(solution)/shard_map/ppermute | solution.py:36
  35.7 162.8 %collective-permute-start.10 = (f32[4,2,8,128]{3,0,2,1:T(4,128)}, f32[4,2,8,128]{3,0,2,1:T(4,128)}, u32[]{:S(2)}, u32[]{:S(2)}) collective-permute-start(f32[4,2,8,128]{3,0,2,1:T(4,128)} %get-tuple-element.245), channel_id=1, source_target_pairs={{0,1},{2,3},{4,5},{6,7},{8,9},{10,11},{12,13},{14,15},{16,17},{18,... | collective-permute-start | bytes 98312 | tf_op jit(solution)/shard_map/ppermute | solution.py:36
  37.9 163.6 %collective-permute-start.11 = (f32[4,2,8,128]{3,0,2,1:T(4,128)}, f32[4,2,8,128]{3,0,2,1:T(4,128)}, u32[]{:S(2)}, u32[]{:S(2)}) collective-permute-start(f32[4,2,8,128]{3,0,2,1:T(4,128)} %get-tuple-element.246), channel_id=1, source_target_pairs={{1,0},{3,2},{5,4},{7,6},{9,8},{11,10},{13,12},{15,14},{17,16},{19,... | collective-permute-start | bytes 98312 | tf_op jit(solution)/shard_map/ppermute | solution.py:39
  41.4 14.4 %copy-start.19 = (f32[6,64,1,8]{1,3,2,0:T(8,128)}, f32[6,64,1,8]{1,3,2,0:T(8,128)S(1)}, u32[]{:S(2)}) copy-start(f32[6,64,1,8]{1,3,2,0:T(8,128)S(1)} %collective-permute-done.1) | copy-start | bytes 36868
  41.5 13.7 %collective-permute-start.3 = (f32[6,64,10,1]{1,3,2,0:T(1,128)S(1)}, f32[6,64,10,1]{1,3,2,0:T(1,128)S(1)}, u32[]{:S(2)}, u32[]{:S(2)}) collective-permute-start(f32[6,64,10,1]{1,3,2,0:T(1,128)S(1)} %get-tuple-element.256), channel_id=1, source_target_pairs={{0,2},{2,4},{4,6},{6,8},{8,10},{10,12},{12,14},{14,16},{16,18},{18... | collective-permute-start | bytes 46088 | tf_op jit(solution)/shard_map/ppermute | solution.py:36
  44.5 10.7 %collective-permute-start.2 = (f32[6,64,10,1]{1,3,2,0:T(1,128)S(1)}, f32[6,64,10,1]{1,3,2,0:T(1,128)S(1)}, u32[]{:S(2)}, u32[]{:S(2)}) collective-permute-start(f32[6,64,10,1]{1,3,2,0:T(1,128)S(1)} %get-tuple-element.255), channel_id=1, source_target_pairs={{2,0},{4,2},{6,4},{8,6},{10,8},{12,10},{14,12},{16,14},{18,16},{20... | collective-permute-start | bytes 46088 | tf_op jit(solution)/shard_map/ppermute | solution.py:39
  55.2 27.3 %copy-start.18 = (f32[6,64,10,1]{1,3,2,0:T(1,128)}, f32[6,64,10,1]{1,3,2,0:T(1,128)S(1)}, u32[]{:S(2)}) copy-start(f32[6,64,10,1]{1,3,2,0:T(1,128)S(1)} %collective-permute-done.3) | copy-start | bytes 46084
  55.2 29.2 %copy-start.16 = (f32[6,64,10,1]{1,3,2,0:T(1,128)}, f32[6,64,10,1]{1,3,2,0:T(1,128)S(1)}, u32[]{:S(2)}) copy-start(f32[6,64,10,1]{1,3,2,0:T(1,128)S(1)} %collective-permute-done.2) | copy-start | bytes 46084
  55.2 203.1 %copy-start.3 = (f32[64,8,8]{0,2,1:T(8,128)}, f32[64,8,8]{0,2,1:T(8,128)S(1)}, u32[]{:S(2)}) copy-start(f32[64,8,8]{0,2,1:T(8,128)S(1)} %fusion.61) | copy-start | bytes 49156
  82.4 28.7 %collective-permute-start.7 = (f32[64,8,1]{0,2,1:T(1,128)}, f32[64,8,1]{0,2,1:T(1,128)S(1)}, u32[]{:S(2)}, u32[]{:S(2)}) collective-permute-start(f32[64,8,1]{0,2,1:T(1,128)} %slice.461), channel_id=1, source_target_pairs={{0,2},{2,4},{4,6},{6,8},{8,10},{10,12},{12,14},{14,16},{16,18},{18... | collective-permute-start | bytes 6152 | tf_op jit(solution)/shard_map/ppermute | solution.py:47
  85.2 88.8 %copy-start.5 = (f32[64,8,8]{0,2,1:T(8,128)}, f32[64,8,8]{0,2,1:T(8,128)S(1)}, u32[]{:S(2)}) copy-start(f32[64,8,8]{0,2,1:T(8,128)S(1)} %fusion.73) | copy-start | bytes 49156
  85.2 32.3 %collective-permute-start.4 = (f32[64,1,8]{0,2,1:T(8,128)S(1)}, f32[64,1,8]{0,2,1:T(8,128)S(1)}, u32[]{:S(2)}, u32[]{:S(2)}) collective-permute-start(f32[64,1,8]{0,2,1:T(8,128)S(1)} %slice.454), channel_id=1, source_target_pairs={{0,32},{32,64},{64,96},{96,128},{128,160},{160,192},{192,224},{224... | collective-permute-start | bytes 6152 | tf_op jit(solution)/shard_map/ppermute | solution.py:47
  111.1 31.3 %copy-start.22 = (pred[64]{0:T(512)(128)(4,1)S(1)}, pred[64]{0:T(512)(128)(4,1)}, u32[]{:S(2)}) copy-start(pred[64]{0:T(512)(128)(4,1)} %add_compare_fusion) | copy-start | bytes 196
  111.1 31.5 %collective-permute-start.6 = (f32[6,1,10,10]{1,0,3,2:T(8,128)}, f32[6,1,10,10]{1,0,3,2:T(8,128)}, u32[]{:S(2)}, u32[]{:S(2)}) collective-permute-start(f32[6,1,10,10]{1,0,3,2:T(8,128)} %get-tuple-element.250), channel_id=1, source_target_pairs={{1,0},{0,1},{3,2},{2,3},{5,4},{4,5},{7,6},{6,7},{9,8},{8,9},{11,10... | collective-permute-start | bytes 7208 | tf_op jit(solution)/shard_map/ppermute | solution.py:39
  117.5 27.0 %collective-permute-start.5 = (f32[6,1,10,10]{1,0,3,2:T(8,128)S(1)}, f32[6,1,10,10]{1,0,3,2:T(8,128)}, u32[]{:S(2)}, u32[]{:S(2)}) collective-permute-start(f32[6,1,10,10]{1,0,3,2:T(8,128)S(1)} %get-tuple-element.249), channel_id=1, source_target_pairs={{0,1},{1,0},{2,3},{3,2},{4,5},{5,4},{6,7},{7,6},{8,9},{9,8},{10,11... | collective-permute-start | bytes 7208 | tf_op jit(solution)/shard_map/ppermute | solution.py:36
  142.6 62.6 %collective-permute-start.9 = (f32[4,64,2,128]{3,0,2,1:T(4,128)}, f32[4,64,2,128]{3,0,2,1:T(4,128)}, u32[]{:S(2)}, u32[]{:S(2)}) collective-permute-start(f32[4,64,2,128]{3,0,2,1:T(4,128)} %get-tuple-element.242), channel_id=1, source_target_pairs={{32,0},{64,32},{96,64},{128,96},{160,128},{192,160},{224,192},{256... | collective-permute-start | bytes 786440 | tf_op jit(solution)/shard_map/ppermute | solution.py:39
  211.8 34.7 %collective-permute-start.15 = (f32[4,2,8,128]{3,0,2,1:T(4,128)S(1)}, f32[4,2,8,128]{3,0,2,1:T(4,128)S(1)}, u32[]{:S(2)}, u32[]{:S(2)}) collective-permute-start(f32[4,2,8,128]{3,0,2,1:T(4,128)S(1)} %get-tuple-element.236), channel_id=1, source_target_pairs={{1,0},{3,2},{5,4},{7,6},{9,8},{11,10},{13,12},{15,14},{17,16},{19,... | collective-permute-start | bytes 98312 | tf_op jit(solution)/shard_map/ppermute | solution.py:39
  213.1 33.4 %collective-permute-start.14 = (f32[4,2,8,128]{3,0,2,1:T(4,128)S(1)}, f32[4,2,8,128]{3,0,2,1:T(4,128)S(1)}, u32[]{:S(2)}, u32[]{:S(2)}) collective-permute-start(f32[4,2,8,128]{3,0,2,1:T(4,128)S(1)} %get-tuple-element.235), channel_id=1, source_target_pairs={{0,1},{2,3},{4,5},{6,7},{8,9},{10,11},{12,13},{14,15},{16,17},{18,... | collective-permute-start | bytes 98312 | tf_op jit(solution)/shard_map/ppermute | solution.py:36
  218.6 31.2 %collective-permute-start.13 = (f32[4,64,2,128]{3,0,2,1:T(4,128)S(1)}, f32[4,64,2,128]{3,0,2,1:T(4,128)S(1)}, u32[]{:S(2)}, u32[]{:S(2)}) collective-permute-start(f32[4,64,2,128]{3,0,2,1:T(4,128)S(1)} %get-tuple-element.232), channel_id=1, source_target_pairs={{32,0},{64,32},{96,64},{128,96},{160,128},{192,160},{224,192},{256... | collective-permute-start | bytes 786440 | tf_op jit(solution)/shard_map/ppermute | solution.py:39
  236.8 13.0 %collective-permute-start.12 = (f32[4,64,2,128]{3,0,2,1:T(4,128)S(1)}, f32[4,64,2,128]{3,0,2,1:T(4,128)S(1)}, u32[]{:S(2)}, u32[]{:S(2)}) collective-permute-start(f32[4,64,2,128]{3,0,2,1:T(4,128)S(1)} %get-tuple-element.231), channel_id=1, source_target_pairs={{0,32},{32,64},{64,96},{96,128},{128,160},{160,192},{192,224},{224... | collective-permute-start | bytes 786440 | tf_op jit(solution)/shard_map/ppermute | solution.py:36
  257.2 172.9 %all-gather.5.cloned.1.call-start = ((), (), s32[]{:S(2)}) async-start(), calls=%async_computation.2 | async-start | bytes 8912896 | tf_op jit(solution)/shard_map/all_gather | solution.py:198
  258.2 68.9 %copy-start.7 = (f32[64,8,8]{0,2,1:T(8,128)S(1)}, f32[64,8,8]{0,2,1:T(8,128)}, u32[]{:S(2)}) copy-start(f32[64,8,8]{0,2,1:T(8,128)} %param.15) | copy-start | bytes 49156
  258.2 68.9 %copy-start.14 = (f32[64,9,8]{0,2,1:T(8,128)S(1)}, f32[64,9,8]{0,2,1:T(8,128)}, u32[]{:S(2)}) copy-start(f32[64,9,8]{0,2,1:T(8,128)} %get-tuple-element.260) | copy-start | bytes 55300
  313.7 13.4 %copy-start.8 = (f32[64,8,8]{0,1,2:T(8,128)S(1)}, f32[64,8,8]{0,1,2:T(8,128)}, u32[]{:S(2)}) copy-start(f32[64,8,8]{0,1,2:T(8,128)} %reduce-scatter.2.cloned.1.call-done) | copy-start | bytes 49156
  (12 other events, 52.9 us)
Sparse Core Ops, SparseCore 0:
  257.3 56.3 reduce-scatter.1
  315.8 114.2 all-gather.4
where the time goes:
time: 447 us; the launch traced here: 446 us
  waiting for transfers between devices  157 us (35%)
  blocking collectives  99.9 us (22%)
  starting transfers between devices  79.7 us (18%)
  other arithmetic  63.8 us (14%)
  local copies, waits for them, and re-layouts  22.5 us (5%)
  between operations  14.9 us (3%)
  matrix products  8.09 us (2%)
    all_gather x1, waiting for transfers between devices, shards(): lax.all_gather(rounded, 'trc', axis=0, tiled=True)  102 us
    reduce_scatter x1, waiting for transfers between devices, shards(): lax.psum_scatter(partial_sum, 'trc', scatter_dimension=2, tiled=True)  54.5 us
    ppermute x7, starting transfers between devices, extended(): lax.ppermute(lax.slice_in_dim(block, 0, width, axis=dim), axis, backward)  47.8 us
    add x6, other arithmetic, limited_div(): jnp.maximum(face_speed, 0.0) * plus_side  31.4 us
    all_gather x3, blocking collectives, entering(): gathered = lax.all_gather(part, axis)  26.2 us
    all_gather x1, blocking collectives, shards(): lax.all_gather(faces_vertical, 'trc', axis=2, tiled=True)  25.7 us
    all_gather x1, blocking collectives, shards(): lax.all_gather(meridional_speed_final, 'trc', axis=2, tiled=True)  24.9 us
    all_gather x1, blocking collectives, shards(): lax.all_gather(faces_east, 'trc', axis=2, tiled=True)  23.1 us
  transfers between devices with their start and end apart: 18, of which 2 were waited for; matrix products, arithmetic and copies ran while one was open for 14% of the time, Pallas kernels for 0%

commit v1 on v0

v1 whole, which is shorter than its diff:
```python
import functools

import jax
import jax.numpy as jnp
from jax import lax
from jax.experimental import pallas as pl
from jax.experimental.pallas import tpu as pltpu
from jax.sharding import PartitionSpec as P

MESH = pl.DeviceIdType.MESH
F32 = jnp.float32
BF16 = jnp.bfloat16
VMEM = pl.BlockSpec(memory_space=pltpu.VMEM)

viscosity = 0.2
buoyancy = 0.25
marine_advance = 0.05
tracer_step = 0.2
level_step = 0.04
react_step = 0.25
warming_amount = 60.0

LOW, AUX, HIGH = 0, 1024, 1152
BLOCK = 2176
PART = 1152


def sds(shape, dtype=F32):
    return jax.ShapeDtypeStruct(shape, dtype)


def iota(shape, axis):
    return lax.broadcasted_iota(jnp.int32, shape, axis)


def pieces(value):
    first = value.astype(BF16)
    rest = value - first.astype(F32)
    second = rest.astype(BF16)
    third = (rest - second.astype(F32)).astype(BF16)
    return first, second, third


def minmod_half(left, right):
    return jnp.maximum(jnp.minimum(left, right), jnp.minimum(jnp.maximum(left, right), 0.0))


def pack_kernel(t_ref, s_ref, u_ref, v_ref, m_ref, above_ref, sp_ref, b_ref, xs_ref):
    for f, ref in enumerate((t_ref, s_ref, u_ref, v_ref)):
        for k in range(4):
            off = (LOW if k < 2 else HIGH) + f * 256 + (k % 2) * 128
            b_ref[:, off : off + 128] = jnp.concatenate([ref[2 * k], ref[2 * k + 1]], axis=1)
    lane = iota((8, 128), 1)
    aux = above_ref[...]
    for x in range(8):
        count = jnp.sum(m_ref[x].astype(F32), axis=1, keepdims=True)
        aux = aux + jnp.where(lane == x, count, 0.0)
    b_ref[:, AUX : AUX + 128] = aux

    def one(t, carry):
        for x in range(8):
            xs_ref[t, x] = sp_ref[t, pl.ds(x, 64, stride=8), :]
        return carry

    lax.fori_loop(0, 4, one, 0)


def gather_kernel(nz, nx, b_ref, xs_ref, g_ref, gl_ref, gh_ref, se_ref, zs, zr, ls, lr, hs, hr, ss, sr):
    z, x, lev = lax.axis_index("trc"), lax.axis_index("cols"), lax.axis_index("lev")
    zup, zdn = {"trc": (z + 1) % nz}, {"trc": (z + nz - 1) % nz}
    xup, xdn = {"cols": (x + 1) % nx}, {"cols": (x + nx - 1) % nx}
    peer = {"lev": 1 - lev}
    barrier = pltpu.get_barrier_semaphore()
    for other in (zup, zdn, xup, xdn, peer):
        pl.semaphore_signal(barrier, inc=1, device_id=other, device_id_type=MESH)
    pl.semaphore_wait(barrier, 5)

    def rdma(src, dst, send, recv, to):
        return pltpu.make_async_remote_copy(
            src_ref=src, dst_ref=dst, send_sem=send, recv_sem=recv, device_id=to, device_id_type=MESH
        )

    def along(src, source, way):
        return rdma(src, g_ref.at[source], zs.at[way, source], zr.at[source], zup if way == 0 else zdn)

    def to_right(src, source):
        return rdma(src.at[:, AUX:], gl_ref.at[source], ls.at[source], lr.at[source], xup)

    def to_left(src, source):
        return rdma(src.at[:, :PART], gh_ref.at[source], hs.at[source], hr.at[source], xdn)

    along(b_ref, z, 0).start()
    along(b_ref, z, 1).start()
    to_right(b_ref, z).start()
    to_left(b_ref, z).start()

    near = pl.multiple_of((1 - lev) * 56, 8)
    there = pl.multiple_of((1 - lev) * 0 + lev * 72, 8)
    nothing = pl.multiple_of(lev * 72, 8)
    own_x = rdma(xs_ref.at[:, 4:8], se_ref.at[:, 0:4, 8:72], ss.at[0], sr.at[0], xup)
    own_y = rdma(xs_ref.at[:, 0:4], se_ref.at[:, 12:16, 8:72], ss.at[1], sr.at[1], xdn)
    own_l = rdma(xs_ref.at[:, :, pl.ds(near, 8)], se_ref.at[:, 4:12, pl.ds(there, 8)], ss.at[2], sr.at[2], peer)
    own_x.start()
    own_y.start()
    own_l.start()

    g_ref[z] = b_ref[...]

    def keep(t, carry):
        se_ref[t, 4:12, 8:72, :] = xs_ref[t]
        se_ref[t, :, pl.ds(nothing, 8), :] = jnp.zeros((16, 8, 128), F32)
        return carry

    lax.fori_loop(0, 4, keep, 0)

    near_e = pl.multiple_of(near + 8, 8)
    low_l = rdma(se_ref.at[:, 0:4, pl.ds(near_e, 8)], se_ref.at[:, 0:4, pl.ds(there, 8)], ss.at[3], sr.at[3], peer)
    high_l = rdma(se_ref.at[:, 12:16, pl.ds(near_e, 8)], se_ref.at[:, 12:16, pl.ds(there, 8)], ss.at[4], sr.at[4], peer)

    half = nz // 2
    for step in range(1, half + 1):
        source = (z + nz - step) % nz
        block = g_ref.at[source]
        along(block, source, 0).wait_recv()
        if step < half:
            along(block, source, 0).start()
        to_right(block, source).start()
        to_left(block, source).start()
        if step < half:
            source = (z + step) % nz
            block = g_ref.at[source]
            along(block, source, 1).wait_recv()
            if step < half - 1:
                along(block, source, 1).start()
            to_right(block, source).start()
            to_left(block, source).start()
        if step == half // 2:
            own_x.wait_recv()
            low_l.start()
            own_y.wait_recv()
            high_l.start()

    own_l.wait_recv()
    low_l.wait_recv()
    high_l.wait_recv()

    def arrived(source, carry):
        to_right(b_ref, source).wait_recv()
        to_left(b_ref, source).wait_recv()
        to_right(b_ref, source).wait_send()
        to_left(b_ref, source).wait_send()
        return carry

    lax.fori_loop(0, nz, arrived, 0)
    for step in range(half):
        along(b_ref, (z + nz - step) % nz, 0).wait_send()
    for step in range(half - 1):
        along(b_ref, (z + step) % nz, 1).wait_send()
    for copy in (own_x, own_y, own_l, low_l, high_l):
        copy.wait_send()


def flow_kernel(g_ref, gl_ref, gh_ref, uf_ref, vf_ref, fv_ref, t_ref, s_ref, bnd_ref, rho, uu, vv, pp, cnt, top):
    lev = lax.axis_index("lev")
    fields = (t_ref, s_ref, uu, vv)
    sides = ((gl_ref, 128), (g_ref, LOW), (g_ref, HIGH), (gh_ref, 0))
    for part, (ref, base) in enumerate(sides):
        for f, out in enumerate(fields):
            for k in range(2):
                off = base + f * 256 + k * 128
                r = part * 4 + k * 2
                out[r : r + 2] = ref[:, off : off + 128].T.reshape(2, 64, 128)
    aux, aux_l, aux_h = g_ref[:, AUX:HIGH].T, gl_ref[:, 0:128].T, gh_ref[:, AUX:HIGH].T
    cnt[0:4], cnt[4:12], cnt[12:16] = aux_l[4:8], aux[0:8], aux_h[0:4]
    top[0:4], top[4:12], top[12:16] = aux_l[12:16], aux[8:16], aux_h[8:12]

    row, col = iota((64, 64), 0), iota((64, 64), 1)
    down = jnp.where(col < row, 1.0, jnp.where(col == row, 0.5, 0.0)).astype(BF16)
    down = jnp.concatenate([down] * 3, axis=1)
    deep = jnp.where(col >= row, 1.0, 0.0).astype(BF16)
    deep = jnp.concatenate([deep] * 3, axis=1)
    for r in range(16):
        dense = 0.8 * s_ref[r] - 0.2 * t_ref[r]
        total = jnp.dot(down, jnp.concatenate(pieces(dense), axis=0), preferred_element_type=F32)
        pp[r] = buoyancy * (top[r : r + 1] + total)

    level = iota((64, 128), 0).astype(F32)
    uf_ref[0] = jnp.zeros((64, 128), F32)
    vf_ref[0] = jnp.zeros((64, 128), F32)
    for r in (14, 15):
        uf_ref[r] = jnp.zeros((64, 128), F32)
        vf_ref[r] = jnp.zeros((64, 128), F32)
    for r in range(1, 14):
        here, east = cnt[r : r + 1], cnt[r + 1 : r + 2]
        north = pltpu.roll(jnp.broadcast_to(here, (8, 128)), 127, 1)[0:1]
        p, u, v = pp[r], uu[r], vv[r]
        lap_u = uu[r + 1] + uu[r - 1] + pltpu.roll(u, 127, 1) + pltpu.roll(u, 1, 1) - 4.0 * u
        lap_v = vv[r + 1] + vv[r - 1] + pltpu.roll(v, 127, 1) + pltpu.roll(v, 1, 1) - 4.0 * v
        new_u = u + marine_advance * (p - pp[r + 1] + viscosity * lap_u)
        new_v = v + marine_advance * (p - pltpu.roll(p, 127, 1) + viscosity * lap_v)
        uf_ref[r] = jnp.where(level < jnp.minimum(here, east), new_u, 0.0)
        vf_ref[r] = jnp.where(level < jnp.minimum(here, north), new_v, 0.0)

    zero = jnp.zeros((1, 128), F32)
    first = lev == 0
    for r in range(16):
        if 2 <= r < 14:
            u, v = uf_ref[r], vf_ref[r]
            div = u - uf_ref[r - 1] + v - pltpu.roll(v, 1, 1)
            fv = jnp.dot(deep, jnp.concatenate(pieces(div), axis=0), preferred_element_type=F32)
            fv_ref[r] = fv
            flow = fv[0:1]
        else:
            fv_ref[r] = jnp.zeros((64, 128), F32)
            flow = zero
        u2 = jnp.where(first, uf_ref[r, 62:64], uf_ref[r, 0:2])
        v2 = jnp.where(first, vf_ref[r, 62:64], vf_ref[r, 0:2])
        t1 = jnp.where(first, t_ref[r, 63:64], t_ref[r, 0:1])
        s1 = jnp.where(first, s_ref[r, 63:64], s_ref[r, 0:1])
        bnd_ref[r] = jnp.concatenate([u2, v2, flow, t1, s1, zero], axis=0)


def advect_kernel(
    uf_ref, vf_ref, fv_ref, t_ref, s_ref, bnd_ref, se_ref, adv_ref, send_ref, oc_ref, up, um, vp, vm, fp, fm, q1, ex, tr
):
    z, lev = lax.axis_index("trc"), lax.axis_index("lev")
    first = lev == 0
    sub = iota((8, 128), 0)

    def around(own, above, below):
        return jnp.concatenate(
            [jnp.where(first, 0.0, above), own, jnp.where(first, below, 0.0)], axis=0
        )

    def faces(r, carry):
        edge = bnd_ref[r]
        edge_w = bnd_ref[r - 1]
        pos = pltpu.roll(edge, 6, 0)
        u_ext = around(uf_ref[r], jnp.where(sub >= 6, pos, 0.0), jnp.where(sub < 2, edge, 0.0))
        two = pltpu.roll(edge, 4, 0)
        low = pltpu.roll(edge, 6, 0)
        v_ext = around(vf_ref[r], jnp.where(sub >= 6, two, 0.0), jnp.where(sub < 2, low, 0.0))
        d2 = edge[0:2] - edge_w[0:2] + edge[2:4] - pltpu.roll(edge, 1, 1)[2:4]
        d0, d1 = d2[0:1], d2[1:2]
        flow = jnp.where(first, edge[4:5], 0.0)
        f_own = fv_ref[r] + flow
        above = jnp.where(sub == 7, f_own[0:1] + d1, jnp.where(sub == 6, f_own[0:1] + d1 + d0, 0.0))
        below = jnp.where(
            sub == 0, flow, jnp.where(sub == 1, flow - d0, jnp.where(sub == 2, flow - d0 - d1, 0.0))
        )
        surface = jnp.where((iota((64, 128), 0) == 0) & first, 0.0, f_own)
        f_ext = level_step * around(surface, above, below)
        u_ext = tracer_step * u_ext
        v_ext = tracer_step * v_ext
        up[r], um[r] = jnp.maximum(u_ext, 0.0), jnp.minimum(u_ext, 0.0)
        vp[r], vm[r] = jnp.maximum(v_ext, 0.0), jnp.minimum(v_ext, 0.0)
        fp[r], fm[r] = jnp.maximum(f_ext, 0.0), jnp.minimum(f_ext, 0.0)
        return carry

    lax.fori_loop(1, 14, faces, 0)

    def sweep(load, store, start, stop):
        d_a = 0.5 * (load(start - 1) - load(start - 2))
        d_b = 0.5 * (load(start) - load(start - 1))
        d_c = 0.5 * (load(start + 1) - load(start))
        right = load(start - 1) + minmod_half(d_a, d_b)
        slope = minmod_half(d_b, d_c)
        flux = up[start - 1] * right + um[start - 1] * (load(start) - slope)

        def one(r, carry):
            d_here, right, flux = carry
            q, q_e = load(r), load(r + 1)
            d_next = 0.5 * (load(r + 2) - q_e)
            slope = minmod_half(d_here, d_next)
            flux_e = up[r] * right + um[r] * (q_e - slope)
            change = flux_e - flux
            right_e = q_e + slope
            north = 0.5 * (pltpu.roll(q, 127, 1) - q)
            slope = minmod_half(pltpu.roll(north, 1, 1), north)
            flux_n = vp[r] * (q + slope) + vm[r] * pltpu.roll(q - slope, 127, 1)
            change = change + (flux_n - pltpu.roll(flux_n, 1, 1))
            below = 0.5 * (pltpu.roll(q, 79, 0) - q)
            slope = minmod_half(pltpu.roll(below, 1, 0), below)
            flux_v = fp[r] * pltpu.roll(q + slope, 1, 0) + fm[r] * (q - slope)
            change = change + (pltpu.roll(flux_v, 79, 0) - flux_v)
            store(r, q - change)
            return d_next, right_e, flux_e

        lax.fori_loop(start, stop, one, (d_c, load(start) + slope, flux))

    def tracer(t, carry):
        def first_load(r):
            return se_ref[t, r]

        def first_store(r, value):
            q1[r] = value

        def second_load(r):
            return q1[r]

        def second_store(r, value):
            adv_ref[t, r - 4] = value[8:72]

        sweep(first_load, first_store, 2, 14)
        sweep(second_load, second_store, 4, 12)
        return carry

    lax.fori_loop(0, 4, tracer, 0)

    def pair(tp, carry):
        for k in range(4):
            one = adv_ref[2 * tp, 2 * k : 2 * k + 2].reshape(128, 128).T.reshape(16, 8, 128)
            two = adv_ref[2 * tp + 1, 2 * k : 2 * k + 2].reshape(128, 128).T.reshape(16, 8, 128)
            send_ref[k, :, tp] = jnp.concatenate([one, two], axis=1).astype(BF16)
        return carry

    lax.fori_loop(0, 2, pair, 0)

    mine = pl.multiple_of(z * 8, 8)
    for f, ref in enumerate((t_ref, s_ref)):
        for r in range(3, 13):
            edge = bnd_ref[r][5 + f : 6 + f]
            ex[r] = around(ref[r], jnp.where(sub == 7, edge, 0.0), jnp.where(sub == 0, edge, 0.0))

        def donor(r, flux_w):
            c = ex[r]
            flux = up[r] * c + um[r] * ex[r + 1]
            flux_n = vp[r] * c + vm[r] * pltpu.roll(c, 127, 1)
            flux_v = fp[r] * pltpu.roll(c, 1, 0) + fm[r] * c
            wide = flux - flux_w + (flux_n - pltpu.roll(flux_n, 1, 1))
            tall = pltpu.roll(flux_v, 79, 0) - flux_v
            new = c - (marine_advance / tracer_step) * wide - (marine_advance / level_step) * tall
            q1[r] = new
            return flux

        lax.fori_loop(4, 12, donor, up[3] * ex[3] + um[3] * ex[4])
        for k in range(4):
            both = jnp.concatenate([q1[4 + 2 * k, 8:72], q1[5 + 2 * k, 8:72]], axis=0)
            tr[...] = both.T
            oc_ref[f, :, k * 128 : k * 128 + 128] = tr[pl.ds(mine, 8), :]
    for f, ref in enumerate((uf_ref, vf_ref)):
        for k in range(4):
            tr[...] = ref[4 + 2 * k : 6 + 2 * k].reshape(128, 128).T
            oc_ref[2 + f, :, k * 128 : k * 128 + 128] = tr[pl.ds(mine, 8), :]


def matrix_kernel(c_ref, absorb_ref, w_ref):
    spread = jnp.where(iota((512, 64), 0) // 8 == iota((512, 64), 1), 1.0, 0.0).astype(BF16)
    across = jnp.where(iota((64, 512), 1) // 8 == iota((64, 512), 0), 1.0, 0.0).astype(BF16)
    tall = jnp.dot(spread, c_ref[...], preferred_element_type=F32).astype(BF16)
    wide = jnp.dot(tall, across, preferred_element_type=F32)
    w_ref[0:512] = jnp.where(iota((512, 512), 0) % 8 == iota((512, 512), 1) % 8, wide, 0.0).astype(BF16)
    own = iota((8, 512), 0) == iota((8, 512), 1) % 8
    rows = []
    for part in pieces(absorb_ref[...]):
        line = jnp.dot(part, across, preferred_element_type=F32)
        rows.append(jnp.where(own, line, 0.0))
    rows.append(jnp.zeros((8, 512), F32))
    w_ref[512:544] = jnp.concatenate(rows, axis=0).astype(BF16)


def react_kernel(nz, send_ref, w_ref, back_ref, att_ref, attp_ref, got, res, s1, r1, s2, r2, s3, r3):
    z, lev = lax.axis_index("trc"), lax.axis_index("lev")
    peer = {"lev": 1 - lev}
    barrier = pltpu.get_barrier_semaphore()

    def greet(d, carry):
        pl.semaphore_signal(barrier, inc=1, device_id={"trc": (z + d) % nz}, device_id_type=MESH)
        return carry

    lax.fori_loop(1, nz, greet, 0)
    pl.semaphore_signal(barrier, inc=1, device_id=peer, device_id_type=MESH)
    pl.semaphore_wait(barrier, nz)

    def rdma(src, dst, send, recv, to):
        return pltpu.make_async_remote_copy(
            src_ref=src, dst_ref=dst, send_sem=send, recv_sem=recv, device_id=to, device_id_type=MESH
        )

    def out(c, d):
        to = (z + d) % nz
        return rdma(send_ref.at[c, to], got.at[c, z], s1.at[c, d], r1.at[c, z], {"trc": to})

    def came(c, d):
        source = (z + d) % nz
        return rdma(send_ref.at[c, source], got.at[c, source], s1.at[c, d], r1.at[c, source], {"trc": source})

    def home(c, d):
        to = (z + d) % nz
        return rdma(res.at[c, to], back_ref.at[c, z], s2.at[c, d], r2.at[c, z], {"trc": to})

    def homed(c, d):
        source = (z + d) % nz
        return rdma(res.at[c, source], back_ref.at[c, source], s2.at[c, d], r2.at[c, source], {"trc": source})

    for c in range(4):
        lax.fori_loop(1, nz, lambda d, carry: (out(c, d).start(), carry)[1], 0)
        got[c, z] = send_ref[c, z]
    for c in range(4):
        lax.fori_loop(1, nz, lambda d, carry: (came(c, d).wait_recv(), carry)[1], 0)
        values = jnp.dot(w_ref[...], got[c].reshape(512, 128), preferred_element_type=F32)
        res[c] = values[0:512].reshape(nz, 32, 128)
        att_ref[c] = values[512:520] + values[520:528] + values[528:536]
        lax.fori_loop(1, nz, lambda d, carry: (home(c, d).start(), carry)[1], 0)
        back_ref[c, z] = res[c, z]
    shade = rdma(att_ref, attp_ref, s3, r3, peer)
    shade.start()
    for c in range(4):

        def finish(d, carry):
            homed(c, d).wait_recv()
            out(c, d).wait_send()
            home(c, d).wait_send()
            return carry

        lax.fori_loop(1, nz, finish, 0)
    shade.wait_recv()
    shade.wait_send()


def final_kernel(adv_ref, back_ref, att_ref, attp_ref, oc_ref, m_ref, w_ref, s_ref, u_ref, v_ref, sp_ref):
    lev = lax.axis_index("lev")

    def one(t, carry):
        at = pl.multiple_of(t * 8, 8)
        for c in range(4):
            react = back_ref[c, :, pl.ds(at, 8), :].reshape(128, 128).T
            new = adv_ref[t, 2 * c : 2 * c + 2].reshape(128, 128) + react_step * react
            sp_ref[t, pl.ds(2 * c, 64, stride=8), :] = new[0:64]
            sp_ref[t, pl.ds(2 * c + 1, 64, stride=8), :] = new[64:128]
        return carry

    lax.fori_loop(0, 4, one, 0)
    row, col = iota((128, 128), 0), iota((128, 128), 1)
    same = row // 64 == col // 64
    before = jnp.where(same & (row < col), 1.0, 0.0).astype(BF16)
    every = jnp.where(same & (lev == 1), 1.0, 0.0).astype(BF16)
    sums = jnp.concatenate([before] * 3 + [every] * 3, axis=0)
    for c in range(4):
        att = att_ref[c]
        terms = jnp.concatenate(pieces(att) + pieces(attp_ref[c]), axis=1)
        path = jnp.dot(terms, sums, preferred_element_type=F32)
        caught = jnp.exp(-path) * (1.0 - jnp.exp(-att))
        wet = jnp.concatenate([m_ref[2 * c], m_ref[2 * c + 1]], axis=1).astype(F32)
        lanes = slice(c * 128, c * 128 + 128)
        warm = oc_ref[0, :, lanes] + warming_amount * wet * caught
        for out, value in ((w_ref, warm), (s_ref, oc_ref[1, :, lanes]), (u_ref, oc_ref[2, :, lanes]), (v_ref, oc_ref[3, :, lanes])):
            out[2 * c] = value[:, 0:64]
            out[2 * c + 1] = value[:, 64:128]


def plain(kernel, outs, scratch=(), name=None):
    return pl.pallas_call(
        kernel,
        out_shape=outs,
        out_specs=jax.tree.map(lambda _: VMEM, outs),
        scratch_shapes=list(scratch),
        compiler_params=pltpu.CompilerParams(vmem_limit_bytes=48 << 20),
        name=name,
    )


def shards(
    nz,
    nx,
    potential_warmth,
    saltiness_anomaly,
    zonal_speed,
    meridional_speed,
    marine_indicator,
    species_concentrations,
    coupling_matrix,
    species_guild_number,
    guild_extinction_coefficient,
):
    tiles = [
        jnp.transpose(a, (1, 2, 0))
        for a in (potential_warmth, saltiness_anomaly, zonal_speed, meridional_speed, marine_indicator)
    ]
    dense = jnp.sum(0.8 * tiles[1] - 0.2 * tiles[0], axis=2)
    above = lax.ppermute(dense, "lev", [(0, 1)])
    above = jnp.pad(above.T, ((0, 0), (8, 112)))
    species = species_concentrations.reshape(4, 512, 128)
    block, xs = plain(pack_kernel, (sds((8, BLOCK)), sds((4, 8, 64, 128))), name="pack")(*tiles, above, species)

    dma = pltpu.SemaphoreType.DMA
    gathered, left, right, ext = pl.pallas_call(
        functools.partial(gather_kernel, nz, nx),
        out_shape=(sds((nz, 8, BLOCK)), sds((nz, 8, PART)), sds((nz, 8, PART)), sds((4, 16, 80, 128))),
        in_specs=[VMEM] * 2,
        out_specs=(VMEM,) * 4,
        scratch_shapes=[dma((2, nz)), dma((nz,)), dma((nz,)), dma((nz,)), dma((nz,)), dma((nz,)), dma((5,)), dma((5,))],
        compiler_params=pltpu.CompilerParams(collective_id=0, has_side_effects=True, vmem_limit_bytes=48 << 20),
        name="gather",
    )(block, xs)

    row = sds((16, 64, 128))
    big = pltpu.VMEM((16, 64, 128), F32)
    small = pltpu.VMEM((16, 128), F32)
    uf, vf, fv, t_ext, s_ext, edge = plain(
        flow_kernel, (row, row, row, row, row, sds((16, 8, 128))), [big, big, big, big, small, small], name="flow"
    )(gathered.reshape(128, BLOCK), left.reshape(128, PART), right.reshape(128, PART))
    edge = lax.ppermute(edge, "lev", [(0, 1), (1, 0)])

    tall = pltpu.VMEM((16, 80, 128), F32)
    adv, send, ocean = plain(
        advect_kernel,
        (sds((4, 8, 64, 128)), sds((4, nz, 2, 16, 128), BF16), sds((4, 8, 512))),
        [tall] * 8 + [pltpu.VMEM((128, 128), F32)],
        name="advect",
    )(uf, vf, fv, t_ext, s_ext, edge, ext)

    onehot = species_guild_number[None, :] == lax.broadcasted_iota(jnp.int32, (8, 64), 0)
    absorb = jnp.sum(jnp.where(onehot, guild_extinction_coefficient[:, None], 0.0), axis=0, keepdims=True)
    absorb = jnp.broadcast_to(absorb, (8, 64))
    matrix = plain(matrix_kernel, sds((544, 512), BF16), name="matrix")(coupling_matrix, absorb)

    back, att, attp = pl.pallas_call(
        functools.partial(react_kernel, nz),
        out_shape=(sds((4, nz, 32, 128)), sds((4, 8, 128)), sds((4, 8, 128))),
        in_specs=[VMEM] * 2,
        out_specs=(VMEM,) * 3,
        scratch_shapes=[
            pltpu.VMEM((4, nz, 2, 16, 128), BF16),
            pltpu.VMEM((4, nz, 32, 128), F32),
            dma((4, nz)),
            dma((4, nz)),
            dma((4, nz)),
            dma((4, nz)),
            dma,
            dma,
        ],
        compiler_params=pltpu.CompilerParams(collective_id=1, has_side_effects=True, vmem_limit_bytes=48 << 20),
        name="react",
    )(send, matrix)

    tile = sds((8, 8, 64))
    warm, salt, zonal, merid, final = plain(
        final_kernel, (tile, tile, tile, tile, sds((4, 512, 128))), name="final"
    )(adv, back, att, attp, ocean, tiles[4])
    warm, salt, zonal, merid = (jnp.transpose(a, (2, 0, 1)) for a in (warm, salt, zonal, merid))
    return warm, salt, zonal, merid, final.reshape(4, 64, 8, 128)


def solution(mesh):
    tile, tracers = P("lev", "cols", "trc"), P("trc", "lev", "cols", None)
    return jax.shard_map(
        functools.partial(shards, mesh.shape["trc"], mesh.shape["cols"]),
        mesh=mesh,
        in_specs=(tile, tile, tile, tile, tile, tracers, P(), P(), P()),
        out_specs=(tile, tile, tile, tile, tracers),
        check_vma=False,
    )
```

time: 447 us -> 184 us (0.41)
  Pallas kernels: 0 us -> 160 us
  waiting for transfers between devices: 157 us -> 3.35 us
  blocking collectives: 99.9 us -> 0 us
  starting transfers between devices: 79.7 us -> 9.9 us
  other arithmetic: 63.8 us -> 0.96 us
  local copies, waits for them, and re-layouts: 22.5 us -> 6.68 us
  between operations: 14.9 us -> 0.76 us
  matrix products: 8.09 us -> 0 us
    pallas_call x0 -> x7, Pallas kernels: none -> 160 us  [the longest x1 79.2 us: shards(): pl.pallas_call(functools.partial(react_kernel, nz), out_shape=(sds((4, nz...]
    all_gather x1 -> x0, waiting for transfers between devices: 102 us -> none  [shards(): lax.all_gather(rounded, 'trc', axis=0, tiled=True)]
    all_gather x6 -> x0, blocking collectives: 99.9 us -> none  [the longest x3 26.2 us: entering(): gathered = lax.all_gather(part, axis)]
    ppermute x16 -> x2, starting transfers between devices: 79.7 us -> 9.9 us  [the longest x1 5.62 us: shards(): above = lax.ppermute(dense, 'lev', [(0, 1)])]
    reduce_scatter x1 -> x0, waiting for transfers between devices: 54.5 us -> none  [shards(): lax.psum_scatter(partial_sum, 'trc', scatter_dimension=2, tiled=True)]
    add x12 -> x0, other arithmetic: 33.8 us -> none  [the longest x6 31.4 us: limited_div(): jnp.maximum(face_speed, 0.0) * plus_side]
    another operation x3 -> x0, other arithmetic: 19 us -> none  [the longest x1 6.33 us: shards(): jnp.cumsum(fluid_mass_per_volume, axis=0)]
    dot_general x1 -> x0, matrix products: 8.09 us -> none  [shards(): jnp.einsum('st,tzxy->szxy', own_rows, lax.all_gather(rounded, 'trc', axis...]
  transfers between devices with their start and end apart: 18 -> 2, of which waited for: 2 -> 2; matrix products, arithmetic and copies ran while one was open for 14% -> 0% of each run, Pallas kernels for 0% -> 0%
where the time goes in v1:
time: 184 us; the launch traced here: 182 us
  Pallas kernels  160 us (87%)
  starting transfers between devices  9.9 us (5%)
  local copies, waits for them, and re-layouts  6.68 us (4%)
  waiting for transfers between devices  3.35 us (2%)
    pallas_call x1, Pallas kernels, shards(): pl.pallas_call(functools.partial(react_kernel, nz), out_shape=(sds((4, nz...  79.2 us
    pallas_call x1, Pallas kernels, shards(): pl.pallas_call(functools.partial(gather_kernel, nz, nx), out_shape=(sds((...  46.9 us
    pallas_call x1, Pallas kernels, shards(): plain(advect_kernel, (sds((4, 8, 64, 128)), sds((4, nz, 2, 16, 128), BF16...  29.8 us
    unnamed x22, local copies, waits for them, and re-layouts  6.53 us
    ppermute x1, starting transfers between devices, shards(): above = lax.ppermute(dense, 'lev', [(0, 1)])  5.62 us
    ppermute x1, starting transfers between devices, shards(): edge = lax.ppermute(edge, 'lev', [(0, 1), (1, 0)])  4.28 us
  transfers between devices with their start and end apart: 2, of which 2 were waited for; matrix products, arithmetic and copies ran while one was open for 0% of the time, Pallas kernels for 0%

profile of v1, /device:TPU:1, one launch (start us, length us, event | category | flops | bytes accessed | tf_op | source)
XLA Modules:
  0.0 181.8 jit_solution(9586995949292421132)
XLA Ops:
  0.6 0.0 copy-start.10
  0.6 0.0 copy-start.9
  0.7 0.0 copy-start.8
  0.7 0.9 subtract_reduce_fusion
  1.5 0.1 copy.15
  1.6 5.6 %collective-permute-start = (f32[8,8]{0,1:T(8,128)S(1)}, f32[8,8]{0,1:T(8,128)S(1)}, u32[]{:S(2)}, u32[]{:S(2)}) collective-permute-start(f32[8,8]{0,1:T(8,128)S(1)} %copy.15), channel_id=1, source_target_pairs={{0,1},{2,3},{4,5},{6,7},{8,9},{10,11},{12,13},{14,15},{16,17},{18,... | collective-permute-start | bytes 776 | tf_op jit(solution)/shard_map/ppermute | solution.py:481
  7.2 0.7 collective-permute-done
  8.0 0.1 pad.4.above_ref
  8.1 0.0 copy-start.1
  8.1 1.2 copy-done.1
  9.3 0.0 copy-start.2
  9.3 0.8 copy-done.2
  10.0 0.8 copy-done.4
  10.8 0.8 copy-done.5
  11.6 0.8 copy-done.6
  12.3 0.8 copy-done.7
  13.1 0.3 pack.1
  13.4 46.9 %gather.1 = (f32[16,8,2176]{2,1,0:T(8,128)S(1)}, f32[16,8,1152]{2,1,0:T(8,128)S(1)}, f32[16,8,1152]{2,1,0:T(8,128)S(1)}, f32[4,16,80,128]{3,2,1,0:T(8,128)S(1)}) custom-call(f32[8,2176]{1,0:T(8,128)S(1)} %get-tuple-element.28.b_ref, f32[4,8,64,128]{3,2,1,0:T(8,128)S(1)} %get-tuple-element.29.xs_ref), custom_call_target="tpu_custom_call" | custom-call | tf_op jit(solution)/shard_map/gather/pallas_call | solution.py:487
  60.3 0.0 copy-start
  60.3 1.5 copy-done
  61.8 1.8 flow.1
  63.6 4.3 %collective-permute-start.1 = (f32[16,8,128]{2,1,0:T(8,128)S(1)}, f32[16,8,128]{2,1,0:T(8,128)S(1)}, u32[]{:S(2)}, u32[]{:S(2)}) collective-permute-start(f32[16,8,128]{2,1,0:T(8,128)S(1)} %get-tuple-element.38), channel_id=1, source_target_pairs={{0,1},{1,0},{2,3},{3,2},{4,5},{5,4},{6,7},{7,6},{8,9},{9,8},{10,11... | collective-permute-start | bytes 196616 | tf_op jit(solution)/shard_map/ppermute | solution.py:503
  67.9 0.0 copy-done.10
  67.9 0.0 copy-done.9
  67.9 0.1 select_reduce_fusion
  68.0 0.0 copy-done.8
  68.0 0.4 matrix.1.w_ref
  68.4 2.6 %collective-permute-done.1.bnd_ref = f32[16,8,128]{2,1,0:T(8,128)S(1)} collective-permute-done((f32[16,8,128]{2,1,0:T(8,128)S(1)}, f32[16,8,128]{2,1,0:T(8,128)S(1)}, u32[]{:S(2)}, u32[]{:S(2)}) %collective-permute-start.1) | collective-permute-done | bytes 65568 | tf_op jit(solution)/shard_map/ppermute | solution.py:503
  71.0 29.8 %advect.1 = (f32[4,8,64,128]{3,2,1,0:T(8,128)S(1)}, bf16[4,16,2,16,128]{4,3,2,1,0:T(8,128)(2,1)S(1)}, f32[4,8,512]{2,1,0:T(8,128)S(1)}) custom-call(f32[16,64,128]{2,1,0:T(8,128)S(1)} %get-tuple-element.33.uf_ref, f32[16,64,128]{2,1,0:T(8,128)S(1)} %get-tuple-element.34.vf_ref, f32[16,64,128]{2,1,0:T(8,128)S(1)} %get-tuple-element.35.fv_ref, ...), custom_call_target="tpu_custom_call" | custom-call | tf_op jit(solution)/shard_map/advect/pallas_call | solution.py:506
  100.8 79.2 %react.1 = (f32[4,16,32,128]{3,2,1,0:T(8,128)S(1)}, f32[4,8,128]{2,1,0:T(8,128)S(1)}, f32[4,8,128]{2,1,0:T(8,128)S(1)}) custom-call(bf16[4,16,2,16,128]{4,3,2,1,0:T(8,128)(2,1)S(1)} %get-tuple-element.41.send_ref, bf16[544,512]{1,0:T(8,128)(2,1)S(1)} %matrix.1.w_ref), custom_call_target="tpu_custom_call" | custom-call | tf_op jit(solution)/shard_map/react/pallas_call | solution.py:518
  180.0 0.0 copy-done.3
  180.0 1.7 final.1
  (6 shorter events, 0.0 us)
Async XLA Ops:
  0.6 67.2 %copy-start.10 = (s32[64]{0:T(128)S(1)}, s32[64]{0:T(128)}, u32[]{:S(2)}) copy-start(s32[64]{0:T(128)} %param.16) | copy-start | bytes 772
  0.6 67.2 %copy-start.9 = (f32[8]{0:T(128)S(1)}, f32[8]{0:T(128)}, u32[]{:S(2)}) copy-start(f32[8]{0:T(128)} %param.17) | copy-start | bytes 100
  0.7 67.3 %copy-start.8 = (bf16[64,64]{1,0:T(8,128)(2,1)S(1)}, bf16[64,64]{1,0:T(8,128)(2,1)}, u32[]{:S(2)}) copy-start(bf16[64,64]{1,0:T(8,128)(2,1)} %c_ref.1) | copy-start | bytes 24580
  1.6 6.4 %collective-permute-start = (f32[8,8]{0,1:T(8,128)S(1)}, f32[8,8]{0,1:T(8,128)S(1)}, u32[]{:S(2)}, u32[]{:S(2)}) collective-permute-start(f32[8,8]{0,1:T(8,128)S(1)} %copy.15), channel_id=1, source_target_pairs={{0,1},{2,3},{4,5},{6,7},{8,9},{10,11},{12,13},{14,15},{16,17},{18,... | collective-permute-start | bytes 776 | tf_op jit(solution)/shard_map/ppermute | solution.py:481
  8.1 1.2 copy-start.1
  9.3 0.8 copy-start.2
  10.0 0.8 copy-start.4
  10.8 0.8 copy-start.5
  11.6 0.8 copy-start.6
  12.3 0.8 copy-start.7
  60.3 1.5 copy-start
  63.6 7.4 %collective-permute-start.1 = (f32[16,8,128]{2,1,0:T(8,128)S(1)}, f32[16,8,128]{2,1,0:T(8,128)S(1)}, u32[]{:S(2)}, u32[]{:S(2)}) collective-permute-start(f32[16,8,128]{2,1,0:T(8,128)S(1)} %get-tuple-element.38), channel_id=1, source_target_pairs={{0,1},{1,0},{2,3},{3,2},{4,5},{5,4},{6,7},{7,6},{8,9},{9,8},{10,11... | collective-permute-start | bytes 196616 | tf_op jit(solution)/shard_map/ppermute | solution.py:503
  71.0 109.0 %copy-start.3 = (s32[64,8,8]{0,2,1:T(8,128)S(1)}, s32[64,8,8]{0,2,1:T(8,128)}, u32[]{:S(2)}) copy-start(s32[64,8,8]{0,2,1:T(8,128)} %param.13) | copy-start | bytes 49156

commit v2 on v1

--- a/solution.py
+++ b/solution.py
@@ -10,6 +10,7 @@
 MESH = pl.DeviceIdType.MESH
 F32 = jnp.float32
 BF16 = jnp.bfloat16
+I16 = jnp.int16
 VMEM = pl.BlockSpec(memory_space=pltpu.VMEM)
 
 viscosity = 0.2
@@ -220,12 +221,68 @@
         bnd_ref[r] = jnp.concatenate([u2, v2, flow, t1, s1, zero], axis=0)
 
 
-def advect_kernel(
-    uf_ref, vf_ref, fv_ref, t_ref, s_ref, bnd_ref, se_ref, adv_ref, send_ref, oc_ref, up, um, vp, vm, fp, fm, q1, ex, tr
+def matrix_kernel(c_ref, absorb_ref, w_ref):
+    place, across = iota((512, 64), 0), iota((64, 512), 1)
+    spread = jnp.where(place // 8 % 16 * 4 + place // 128 == iota((512, 64), 1), 1.0, 0.0).astype(BF16)
+    across = jnp.where(across // 8 % 16 * 4 + across // 128 == iota((64, 512), 0), 1.0, 0.0).astype(BF16)
+    tall = jnp.dot(spread, c_ref[...], preferred_element_type=F32).astype(BF16)
+    wide = jnp.dot(tall, across, preferred_element_type=F32)
+    w_ref[0:512] = jnp.where(iota((512, 512), 0) % 8 == iota((512, 512), 1) % 8, wide, 0.0).astype(BF16)
+    own = iota((8, 512), 0) == iota((8, 512), 1) % 8
+    rows = []
+    for part in pieces(absorb_ref[...]):
+        line = jnp.dot(part, across, preferred_element_type=F32)
+        rows.append(jnp.where(own, line, 0.0))
+    rows.append(jnp.zeros((8, 512), F32))
+    w_ref[512:544] = jnp.concatenate(rows, axis=0).astype(BF16)
+
+
+def react_kernel(
+    nz, uf_ref, vf_ref, fv_ref, t_ref, s_ref, edge_ref, se_ref, w_ref,
+    adv_ref, back_ref, scale_ref, att_ref, attp_ref, oc_ref,
+    up, um, vp, vm, fp, fm, q1, ex, tr, bnd_ref, send_ref, got, res, sizes,
+    s1, r1, s2, r2, s3, r3, s4, r4,
 ):
     z, lev = lax.axis_index("trc"), lax.axis_index("lev")
     first = lev == 0
     sub = iota((8, 128), 0)
+    peer = {"lev": 1 - lev}
+    barrier = pltpu.get_barrier_semaphore()
+
+    def greet(d, carry):
+        pl.semaphore_signal(barrier, inc=1, device_id={"trc": (z + d) % nz}, device_id_type=MESH)
+        return carry
+
+    lax.fori_loop(1, nz, greet, 0)
+    pl.semaphore_signal(barrier, inc=1, device_id=peer, device_id_type=MESH)
+    pl.semaphore_wait(barrier, nz)
+
+    def rdma(src, dst, send, recv, to):
+        return pltpu.make_async_remote_copy(
+            src_ref=src, dst_ref=dst, send_sem=send, recv_sem=recv, device_id=to, device_id_type=MESH
+        )
+
+    def each(body):
+        lax.fori_loop(1, nz, lambda d, carry: (body((z + d) % nz), carry)[1], 0)
+
+    def out(t, to, at):
+        return rdma(send_ref.at[t, to], got.at[t, at], s1.at[t, to], r1.at[t, at], {"trc": to})
+
+    def home(c, to, at):
+        return rdma(res.at[c, :, to], back_ref.at[c, :, at], s2.at[c, to], r2.at[c, at], {"trc": to})
+
+    def size(c, to, at):
+        return rdma(sizes.at[c, to], scale_ref.at[c, at], s4.at[c, to], r4.at[c, at], {"trc": to})
+
+    edges = rdma(edge_ref.at[1:14], bnd_ref.at[1:14], s3.at[0], r3.at[0], peer)
+    edges.start()
+    mine = pl.multiple_of(z * 8, 8)
+    for f, ref in enumerate((uf_ref, vf_ref)):
+        for k in range(4):
+            tr[...] = ref[4 + 2 * k : 6 + 2 * k].reshape(128, 128).T
+            oc_ref[2 + f, :, k * 128 : k * 128 + 128] = tr[pl.ds(mine, 8), :]
+    bnd_ref[0] = jnp.zeros((8, 128), F32)
+    edges.wait_recv()
 
     def around(own, above, below):
         return jnp.concatenate(
@@ -303,20 +360,15 @@
 
         sweep(first_load, first_store, 2, 14)
         sweep(second_load, second_store, 4, 12)
+        for k in range(4):
+            across = adv_ref[t, 2 * k : 2 * k + 2].reshape(128, 128).T.reshape(16, 8, 128)
+            send_ref[t, :, :, k * 128 : k * 128 + 128] = across.astype(BF16)
+        each(lambda to: out(t, to, z).start())
+        got[t, z] = send_ref[t, z]
         return carry
 
     lax.fori_loop(0, 4, tracer, 0)
 
-    def pair(tp, carry):
-        for k in range(4):
-            one = adv_ref[2 * tp, 2 * k : 2 * k + 2].reshape(128, 128).T.reshape(16, 8, 128)
-            two = adv_ref[2 * tp + 1, 2 * k : 2 * k + 2].reshape(128, 128).T.reshape(16, 8, 128)
-            send_ref[k, :, tp] = jnp.concatenate([one, two], axis=1).astype(BF16)
-        return carry
-
-    lax.fori_loop(0, 2, pair, 0)
-
-    mine = pl.multiple_of(z * 8, 8)
     for f, ref in enumerate((t_ref, s_ref)):
         for r in range(3, 13):
             edge = bnd_ref[r][5 + f : 6 + f]
@@ -338,93 +390,45 @@
             both = jnp.concatenate([q1[4 + 2 * k, 8:72], q1[5 + 2 * k, 8:72]], axis=0)
             tr[...] = both.T
             oc_ref[f, :, k * 128 : k * 128 + 128] = tr[pl.ds(mine, 8), :]
-    for f, ref in enumerate((uf_ref, vf_ref)):
-        for k in range(4):
-            tr[...] = ref[4 + 2 * k : 6 + 2 * k].reshape(128, 128).T
-            oc_ref[2 + f, :, k * 128 : k * 128 + 128] = tr[pl.ds(mine, 8), :]
-
-
-def matrix_kernel(c_ref, absorb_ref, w_ref):
-    spread = jnp.where(iota((512, 64), 0) // 8 == iota((512, 64), 1), 1.0, 0.0).astype(BF16)
-    across = jnp.where(iota((64, 512), 1) // 8 == iota((64, 512), 0), 1.0, 0.0).astype(BF16)
-    tall = jnp.dot(spread, c_ref[...], preferred_element_type=F32).astype(BF16)
-    wide = jnp.dot(tall, across, preferred_element_type=F32)
-    w_ref[0:512] = jnp.where(iota((512, 512), 0) % 8 == iota((512, 512), 1) % 8, wide, 0.0).astype(BF16)
-    own = iota((8, 512), 0) == iota((8, 512), 1) % 8
-    rows = []
-    for part in pieces(absorb_ref[...]):
-        line = jnp.dot(part, across, preferred_element_type=F32)
-        rows.append(jnp.where(own, line, 0.0))
-    rows.append(jnp.zeros((8, 512), F32))
-    w_ref[512:544] = jnp.concatenate(rows, axis=0).astype(BF16)
-
-
-def react_kernel(nz, send_ref, w_ref, back_ref, att_ref, attp_ref, got, res, s1, r1, s2, r2, s3, r3):
-    z, lev = lax.axis_index("trc"), lax.axis_index("lev")
-    peer = {"lev": 1 - lev}
-    barrier = pltpu.get_barrier_semaphore()
-
-    def greet(d, carry):
-        pl.semaphore_signal(barrier, inc=1, device_id={"trc": (z + d) % nz}, device_id_type=MESH)
-        return carry
-
-    lax.fori_loop(1, nz, greet, 0)
-    pl.semaphore_signal(barrier, inc=1, device_id=peer, device_id_type=MESH)
-    pl.semaphore_wait(barrier, nz)
-
-    def rdma(src, dst, send, recv, to):
-        return pltpu.make_async_remote_copy(
-            src_ref=src, dst_ref=dst, send_sem=send, recv_sem=recv, device_id=to, device_id_type=MESH
-        )
-
-    def out(c, d):
-        to = (z + d) % nz
-        return rdma(send_ref.at[c, to], got.at[c, z], s1.at[c, d], r1.at[c, z], {"trc": to})
-
-    def came(c, d):
-        source = (z + d) % nz
-        return rdma(send_ref.at[c, source], got.at[c, source], s1.at[c, d], r1.at[c, source], {"trc": source})
-
-    def home(c, d):
-        to = (z + d) % nz
-        return rdma(res.at[c, to], back_ref.at[c, z], s2.at[c, d], r2.at[c, z], {"trc": to})
-
-    def homed(c, d):
-        source = (z + d) % nz
-        return rdma(res.at[c, source], back_ref.at[c, source], s2.at[c, d], r2.at[c, source], {"trc": source})
-
+
+    lax.fori_loop(0, 4, lambda t, carry: (each(lambda at: out(t, at, at).wait_recv()), carry)[1], 0)
     for c in range(4):
-        lax.fori_loop(1, nz, lambda d, carry: (out(c, d).start(), carry)[1], 0)
-        got[c, z] = send_ref[c, z]
-    for c in range(4):
-        lax.fori_loop(1, nz, lambda d, carry: (came(c, d).wait_recv(), carry)[1], 0)
-        values = jnp.dot(w_ref[...], got[c].reshape(512, 128), preferred_element_type=F32)
-        res[c] = values[0:512].reshape(nz, 32, 128)
+        values = got[:, :, :, c * 128 : c * 128 + 128].reshape(512, 128)
+        values = jnp.dot(w_ref[...], values, preferred_element_type=F32)
         att_ref[c] = values[512:520] + values[520:528] + values[528:536]
-        lax.fori_loop(1, nz, lambda d, carry: (home(c, d).start(), carry)[1], 0)
-        back_ref[c, z] = res[c, z]
-    shade = rdma(att_ref, attp_ref, s3, r3, peer)
+        values = values[0:512].reshape(4, nz, 8, 128)
+        largest = jnp.max(jnp.max(jnp.abs(values), axis=0), axis=1, keepdims=True)
+        largest = jnp.maximum(largest, 1e-30)
+        sizes[c] = largest * (1.0 / 32767.0)
+        coded = jnp.round(values * (32767.0 / largest)[None])
+        res[c] = coded.astype(jnp.int32).astype(I16)
+        each(lambda to: (home(c, to, z).start(), size(c, to, z).start()))
+        back_ref[c, :, z] = res[c, :, z]
+        scale_ref[c, z] = sizes[c, z]
+    shade = rdma(att_ref, attp_ref, s3.at[1], r3.at[1], peer)
     shade.start()
     for c in range(4):
 
-        def finish(d, carry):
-            homed(c, d).wait_recv()
-            out(c, d).wait_send()
-            home(c, d).wait_send()
-            return carry
-
-        lax.fori_loop(1, nz, finish, 0)
+        def finish(at):
+            home(c, at, at).wait_recv()
+            size(c, at, at).wait_recv()
+            out(c, at, at).wait_send()
+            home(c, at, at).wait_send()
+            size(c, at, at).wait_send()
+
+        each(finish)
     shade.wait_recv()
     shade.wait_send()
-
-
-def final_kernel(adv_ref, back_ref, att_ref, attp_ref, oc_ref, m_ref, w_ref, s_ref, u_ref, v_ref, sp_ref):
+    edges.wait_send()
+
+
+def final_kernel(adv_ref, back_ref, scale_ref, att_ref, attp_ref, oc_ref, m_ref, w_ref, s_ref, u_ref, v_ref, sp_ref):
     lev = lax.axis_index("lev")
 
     def one(t, carry):
-        at = pl.multiple_of(t * 8, 8)
         for c in range(4):
-            react = back_ref[c, :, pl.ds(at, 8), :].reshape(128, 128).T
+            react = back_ref[c, t].astype(jnp.int32).astype(F32) * scale_ref[c]
+            react = react.reshape(128, 128).T
             new = adv_ref[t, 2 * c : 2 * c + 2].reshape(128, 128) + react_step * react
             sp_ref[t, pl.ds(2 * c, 64, stride=8), :] = new[0:64]
             sp_ref[t, pl.ds(2 * c + 1, 64, stride=8), :] = new[64:128]
@@ -500,44 +504,44 @@
     uf, vf, fv, t_ext, s_ext, edge = plain(
         flow_kernel, (row, row, row, row, row, sds((16, 8, 128))), [big, big, big, big, small, small], name="flow"
     )(gathered.reshape(128, BLOCK), left.reshape(128, PART), right.reshape(128, PART))
-    edge = lax.ppermute(edge, "lev", [(0, 1), (1, 0)])
-
-    tall = pltpu.VMEM((16, 80, 128), F32)
-    adv, send, ocean = plain(
-        advect_kernel,
-        (sds((4, 8, 64, 128)), sds((4, nz, 2, 16, 128), BF16), sds((4, 8, 512))),
-        [tall] * 8 + [pltpu.VMEM((128, 128), F32)],
-        name="advect",
-    )(uf, vf, fv, t_ext, s_ext, edge, ext)
-
     onehot = species_guild_number[None, :] == lax.broadcasted_iota(jnp.int32, (8, 64), 0)
     absorb = jnp.sum(jnp.where(onehot, guild_extinction_coefficient[:, None], 0.0), axis=0, keepdims=True)
     absorb = jnp.broadcast_to(absorb, (8, 64))
     matrix = plain(matrix_kernel, sds((544, 512), BF16), name="matrix")(coupling_matrix, absorb)
 
-    back, att, attp = pl.pallas_call(
+    tall = pltpu.VMEM((16, 80, 128), F32)
+    adv, back, scale, att, attp, ocean = pl.pallas_call(
         functools.partial(react_kernel, nz),
-        out_shape=(sds((4, nz, 32, 128)), sds((4, 8, 128)), sds((4, 8, 128))),
-        in_specs=[VMEM] * 2,
-        out_specs=(VMEM,) * 3,
-        scratch_shapes=[
-            pltpu.VMEM((4, nz, 2, 16, 128), BF16),
-            pltpu.VMEM((4, nz, 32, 128), F32),
-            dma((4, nz)),
-            dma((4, nz)),
-            dma((4, nz)),
-            dma((4, nz)),
-            dma,
-            dma,
-        ],
+        out_shape=(
+            sds((4, 8, 64, 128)),
+            sds((4, 4, nz, 8, 128), I16),
+            sds((4, nz, 1, 128)),
+            sds((4, 8, 128)),
+            sds((4, 8, 128)),
+            sds((4, 8, 512)),
+        ),
+        in_specs=[VMEM] * 8,
+        out_specs=(VMEM,) * 6,
+        scratch_shapes=[tall] * 8
+        + [
+            pltpu.VMEM((128, 128), F32),
+            pltpu.VMEM((16, 8, 128), F32),
+            pltpu.VMEM((4, nz, 8, 512), BF16),
+            pltpu.VMEM((4, nz, 8, 512), BF16),
+            pltpu.VMEM((4, 4, nz, 8, 128), I16),
+            pltpu.VMEM((4, nz, 1, 128), F32),
+        ]
+        + [dma((4, nz))] * 4
+        + [dma((2,))] * 2
+        + [dma((4, nz))] * 2,
         compiler_params=pltpu.CompilerParams(collective_id=1, has_side_effects=True, vmem_limit_bytes=48 << 20),
         name="react",
-    )(send, matrix)
+    )(uf, vf, fv, t_ext, s_ext, edge, ext, matrix)
 
     tile = sds((8, 8, 64))
     warm, salt, zonal, merid, final = plain(
         final_kernel, (tile, tile, tile, tile, sds((4, 512, 128))), name="final"
-    )(adv, back, att, attp, ocean, tiles[4])
+    )(adv, back, scale, att, attp, ocean, tiles[4])
     warm, salt, zonal, merid = (jnp.transpose(a, (2, 0, 1)) for a in (warm, salt, zonal, merid))
     return warm, salt, zonal, merid, final.reshape(4, 64, 8, 128)
 

time: 184 us -> 144 us (0.78)
  Pallas kernels: 160 us -> 127 us
  starting transfers between devices: 9.9 us -> 5.62 us
  waiting for transfers between devices: 3.35 us -> 0.01 us
    pallas_call x2 -> x1, Pallas kernels: 109 us -> 76.6 us  [shards(): pl.pallas_call(functools.partial(react_kernel, nz), out_shape=(sds((4, 8,...]
    ppermute x1 -> x0, starting transfers between devices: 4.28 us -> none  [shards(): edge = lax.ppermute(edge, 'lev', [(0, 1), (1, 0)])]
    ppermute x1 -> x0, waiting for transfers between devices: 2.61 us -> none  [shards(): edge = lax.ppermute(edge, 'lev', [(0, 1), (1, 0)])]
    unnamed x22 -> x18, local copies, waits for them, and re-layouts: 6.53 us -> 7.24 us
  transfers between devices with their start and end apart: 2 -> 1, of which waited for: 2 -> 0; matrix products, arithmetic and copies ran while one was open for 0% -> 1% of each run, Pallas kernels for 0% -> 0%
where the time goes in v2:
time: 144 us; the launch traced here: 143 us
  Pallas kernels  127 us (88%)
  local copies, waits for them, and re-layouts  7.39 us (5%)
  starting transfers between devices  5.62 us (4%)
  other arithmetic  1.62 us (1%)
    pallas_call x1, Pallas kernels, shards(): pl.pallas_call(functools.partial(react_kernel, nz), out_shape=(sds((4, 8,...  76.6 us
    pallas_call x1, Pallas kernels, shards(): pl.pallas_call(functools.partial(gather_kernel, nz, nx), out_shape=(sds((...  46.5 us
    unnamed x18, local copies, waits for them, and re-layouts  7.24 us
    ppermute x1, starting transfers between devices, shards(): above = lax.ppermute(dense, 'lev', [(0, 1)])  5.62 us
  transfers between devices with their start and end apart: 1, of which 0 were waited for; matrix products, arithmetic and copies ran while one was open for 1% of the time, Pallas kernels for 0%

profile of v2, /device:TPU:1, one launch (start us, length us, event | category | flops | bytes accessed | tf_op | source)
XLA Modules:
  0.0 142.7 jit_solution(4549833417615921600)
XLA Ops:
  0.6 0.9 subtract_reduce_fusion
  1.5 0.1 copy.15
  1.6 5.6 %collective-permute-start = (f32[8,8]{0,1:T(8,128)S(1)}, f32[8,8]{0,1:T(8,128)S(1)}, u32[]{:S(2)}, u32[]{:S(2)}) collective-permute-start(f32[8,8]{0,1:T(8,128)S(1)} %copy.15), channel_id=1, source_target_pairs={{0,1},{2,3},{4,5},{6,7},{8,9},{10,11},{12,13},{14,15},{16,17},{18,... | collective-permute-start | bytes 776 | tf_op jit(solution)/shard_map/ppermute | solution.py:485
  7.2 0.8 select_reduce_fusion
  8.0 0.0 copy-start.8
  8.0 0.7 copy-done.8
  8.7 0.4 matrix.1.w_ref
  9.1 0.0 collective-permute-done
  9.1 0.1 pad.4.above_ref
  9.2 0.0 copy-start.1
  9.2 1.2 copy-done.1
  10.4 0.0 copy-start.2
  10.4 0.8 copy-done.2
  11.2 0.0 copy-start.4
  11.2 0.8 copy-done.4
  11.9 0.0 copy-start.5
  12.0 0.8 copy-done.5
  12.7 0.0 copy-start.6
  12.7 0.8 copy-done.6
  13.5 0.0 copy-start.7
  13.5 0.8 copy-done.7
  14.2 0.3 pack.1
  14.5 46.5 %gather.1 = (f32[16,8,2176]{2,1,0:T(8,128)S(1)}, f32[16,8,1152]{2,1,0:T(8,128)S(1)}, f32[16,8,1152]{2,1,0:T(8,128)S(1)}, f32[4,16,80,128]{3,2,1,0:T(8,128)S(1)}) custom-call(f32[8,2176]{1,0:T(8,128)S(1)} %get-tuple-element.28.b_ref, f32[4,8,64,128]{3,2,1,0:T(8,128)S(1)} %get-tuple-element.29.xs_ref), custom_call_target="tpu_custom_call" | custom-call | tf_op jit(solution)/shard_map/gather/pallas_call | solution.py:491
  61.0 0.0 copy-start
  61.1 1.5 %copy-done = f32[4,16,80,128]{3,2,1,0:T(8,128)} copy-done((f32[4,16,80,128]{3,2,1,0:T(8,128)}, f32[4,16,80,128]{3,2,1,0:T(8,128)S(1)}, u32[]{:S(2)}) %copy-start) | copy-done | bytes 2621464
  62.6 1.8 %flow.1 = (f32[16,64,128]{2,1,0:T(8,128)S(1)}, f32[16,64,128]{2,1,0:T(8,128)S(1)}, f32[16,64,128]{2,1,0:T(8,128)S(1)}, f32[16,64,128]{2,1,0:T(8,128)S(1)}, f32[1...) custom-call(f32[128,2176]{1,0:T(8,128)S(1)} %bitcast.17, f32[128,1152]{1,0:T(8,128)S(1)} %bitcast.19, ...), custom_call_target="tpu_custom_call" | custom-call | tf_op jit(solution)/shard_map/flow/pallas_call | solution.py:504
  64.4 0.0 copy-start.3
  64.4 76.6 %react.1 = (f32[4,8,64,128]{3,2,1,0:T(8,128)S(1)}, s16[4,4,16,8,128]{4,3,2,1,0:T(8,128)(2,1)S(1)}, f32[4,16,1,128]{3,2,1,0:T(1,128)S(1)}, f32[4,8,128]{2,1,0:T(8...) custom-call(f32[16,64,128]{2,1,0:T(8,128)S(1)} %get-tuple-element.33.uf_ref, ...), custom_call_target="tpu_custom_call" | custom-call | tf_op jit(solution)/shard_map/react/pallas_call | solution.py:513
  141.0 0.0 copy-done.3
  141.0 1.8 %final.1 = (f32[8,8,64]{2,1,0:T(8,128)}, f32[8,8,64]{2,1,0:T(8,128)}, f32[8,8,64]{2,1,0:T(8,128)}, f32[8,8,64]{2,1,0:T(8,128)}, f32[4,512,128]{2,1,0:T(8,128)}) custom-call(f32[4,8,64,128]{3,2,1,0:T(8,128)S(1)} %get-tuple-element.40.adv_ref, s16[4,4,16,8,128]{4,3,2,1,0:T(8,128)(2,1)S(1)} %get-tuple-element.41.back_ref, ...), custom_call_target="tpu_custom_call" | custom-call | tf_op jit(solution)/shard_map/final/pallas_call | solution.py:542
  (1 shorter events, 0.0 us)
Async XLA Ops:
  1.6 7.6 %collective-permute-start = (f32[8,8]{0,1:T(8,128)S(1)}, f32[8,8]{0,1:T(8,128)S(1)}, u32[]{:S(2)}, u32[]{:S(2)}) collective-permute-start(f32[8,8]{0,1:T(8,128)S(1)} %copy.15), channel_id=1, source_target_pairs={{0,1},{2,3},{4,5},{6,7},{8,9},{10,11},{12,13},{14,15},{16,17},{18,... | collective-permute-start | bytes 776 | tf_op jit(solution)/shard_map/ppermute | solution.py:485
  8.0 0.7 copy-start.8
  9.2 1.2 copy-start.1
  10.4 0.8 copy-start.2
  11.2 0.8 copy-start.4
  11.9 0.8 copy-start.5
  12.7 0.8 copy-start.6
  13.5 0.8 copy-start.7
  61.0 1.5 %copy-start = (f32[4,16,80,128]{3,2,1,0:T(8,128)}, f32[4,16,80,128]{3,2,1,0:T(8,128)S(1)}, u32[]{:S(2)}) copy-start(f32[4,16,80,128]{3,2,1,0:T(8,128)S(1)} %get-tuple-element.39.se_ref) | copy-start | bytes 7864324
  64.4 76.6 %copy-start.3 = (s32[64,8,8]{0,2,1:T(8,128)S(1)}, s32[64,8,8]{0,2,1:T(8,128)}, u32[]{:S(2)}) copy-start(s32[64,8,8]{0,2,1:T(8,128)} %param.13) | copy-start | bytes 49156

commit v3 on v2

v3 whole, which is shorter than its diff:
```python
import functools

import jax
import jax.numpy as jnp
from jax import lax
from jax.experimental import pallas as pl
from jax.experimental.pallas import tpu as pltpu
from jax.sharding import PartitionSpec as P

MESH = pl.DeviceIdType.MESH
F32 = jnp.float32
BF16 = jnp.bfloat16
I16 = jnp.int16

viscosity = 0.2
buoyancy = 0.25
marine_advance = 0.05
tracer_step = 0.2
level_step = 0.04
react_step = 0.25
warming_amount = 60.0

SPEEDS, WATER = 1024, 1152


def sds(shape, dtype=F32):
    return jax.ShapeDtypeStruct(shape, dtype)


def iota(shape, axis):
    return lax.broadcasted_iota(jnp.int32, shape, axis)


def pieces(value):
    first = value.astype(BF16)
    rest = value - first.astype(F32)
    second = rest.astype(BF16)
    third = (rest - second.astype(F32)).astype(BF16)
    return first, second, third


def minmod_half(left, right):
    return jnp.maximum(jnp.minimum(left, right), jnp.minimum(jnp.maximum(left, right), 0.0))


def gather_kernel(
    nz, nx, t_hbm, s_hbm, u_hbm, v_hbm, m_hbm, sp_hbm,
    ga, gb, la, lb, ha, hb, se,
    t_in, s_in, u_in, v_in, m_in, sp_in, a_own, b_own, d_own, d_peer,
    ins, zs, zr, ls, lr, hs, hr, ss, sr,
):
    z, x, lev = lax.axis_index("trc"), lax.axis_index("cols"), lax.axis_index("lev")
    zup, zdn = {"trc": (z + 1) % nz}, {"trc": (z + nz - 1) % nz}
    xup, xdn = {"cols": (x + 1) % nx}, {"cols": (x + nx - 1) % nx}
    peer = {"lev": 1 - lev}
    loads = [
        pltpu.make_async_copy(src, dst, ins.at[i])
        for i, (src, dst) in enumerate(
            ((u_hbm, u_in), (v_hbm, v_in), (t_hbm, t_in), (s_hbm, s_in), (m_hbm, m_in), (sp_hbm, sp_in))
        )
    ]
    for load in loads:
        load.start()
    barrier = pltpu.get_barrier_semaphore()
    for other in (xup, xdn, peer):
        pl.semaphore_signal(barrier, inc=1, device_id=other, device_id_type=MESH)

    def greet(d, carry):
        pl.semaphore_signal(barrier, inc=1, device_id={"trc": (z + d) % nz}, device_id_type=MESH)
        return carry

    lax.fori_loop(1, nz, greet, 0)

    def rdma(src, dst, send, recv, to):
        return pltpu.make_async_remote_copy(
            src_ref=src, dst_ref=dst, send_sem=send, recv_sem=recv, device_id=to, device_id_type=MESH
        )

    wholes, lefts, rights = (ga, gb), (la, lb), (ha, hb)
    upper, lower = (SPEEDS // 2, 512), (SPEEDS // 2, 640)

    def along(k, src, source, way):
        return rdma(src, wholes[k].at[source], zs.at[k, way, source], zr.at[k, source], zup if way == 0 else zdn)

    def to_right(k, src, source):
        return rdma(src.at[:, upper[k] :], lefts[k].at[source], ls.at[k, source], lr.at[k, source], xup)

    def to_left(k, src, source):
        return rdma(src.at[:, : lower[k]], rights[k].at[source], hs.at[k, source], hr.at[k, source], xdn)

    def fill(block, refs, high):
        for f, ref in enumerate(refs):
            for k in range(4):
                off = (0 if k < 2 else high) + f * 256 + (k % 2) * 128
                block[:, off : off + 128] = jnp.concatenate([ref[2 * k], ref[2 * k + 1]], axis=1)

    def begin(k, block):
        along(k, block, z, 0).start()
        along(k, block, z, 1).start()
        to_right(k, block, z).start()
        to_left(k, block, z).start()
        wholes[k][z] = block[...]

    loads[0].wait()
    loads[1].wait()
    fill(a_own, (u_in, v_in), 512)
    pl.semaphore_wait(barrier, nz + 2)
    begin(0, a_own)

    for load in loads[2:5]:
        load.wait()
    lane = iota((8, 128), 1)
    counts = jnp.zeros((8, 128), F32)
    dense = jnp.zeros((8, 128), F32)
    for i in range(8):
        counts = counts + jnp.where(lane == i, jnp.sum(m_in[i].astype(F32), axis=1, keepdims=True), 0.0)
        column = jnp.sum(0.8 * s_in[i] - 0.2 * t_in[i], axis=1, keepdims=True)
        dense = dense + jnp.where(lane == i + 8, column, 0.0)
    d_own[...] = dense
    above = rdma(d_own, d_peer, ss.at[5], sr.at[5], peer)
    above.start()
    fill(b_own, (t_in, s_in), 640)

    loads[5].wait()

    def spread(t, carry):
        for i in range(8):
            se[t, 4 + i, 8:72, :] = sp_in[t, pl.ds(i, 64, stride=8), :]
        return carry

    lax.fori_loop(0, 4, spread, 0)
    near = pl.multiple_of((1 - lev) * 56 + 8, 8)
    there = pl.multiple_of(lev * 72, 8)
    own_x = rdma(se.at[:, 8:12, 8:72], se.at[:, 0:4, 8:72], ss.at[0], sr.at[0], xup)
    own_y = rdma(se.at[:, 4:8, 8:72], se.at[:, 12:16, 8:72], ss.at[1], sr.at[1], xdn)
    parts = [
        rdma(se.at[:, low:high, pl.ds(near, 8)], se.at[:, low:high, pl.ds(there, 8)], ss.at[i], sr.at[i], peer)
        for i, low, high in ((2, 4, 12), (3, 0, 4), (4, 12, 16))
    ]
    above.wait_recv()
    b_own[:, 512:640] = counts + jnp.where(lev == 1, d_peer[...], 0.0)
    begin(1, b_own)
    own_x.start()
    own_y.start()
    parts[0].start()

    def clear(t, carry):
        se[t, :, pl.ds(there, 8), :] = jnp.zeros((16, 8, 128), F32)
        return carry

    lax.fori_loop(0, 4, clear, 0)
    half = nz // 2
    for step in range(1, half + 1):
        came = []
        for k in range(2):
            for way, source in ((0, (z + nz - step) % nz), (1, (z + step) % nz))[: 2 if step < half else 1]:
                block = wholes[k].at[source]
                along(k, block, source, way).wait_recv()
                if step < half - way:
                    along(k, block, source, way).start()
                came.append((k, block, source))
        for k, block, source in came:
            to_right(k, block, source).start()
            to_left(k, block, source).start()
        if step == 3:
            own_x.wait_recv()
            parts[1].start()
            own_y.wait_recv()
            parts[2].start()

    for part in parts:
        part.wait_recv()
        part.wait_send()

    for k, block in ((0, a_own), (1, b_own)):

        def arrived(source, carry):
            to_right(k, block, source).wait_recv()
            to_left(k, block, source).wait_recv()
            to_right(k, block, source).wait_send()
            to_left(k, block, source).wait_send()
            return carry

        lax.fori_loop(0, nz, arrived, 0)
        for step in range(half):
            along(k, block, (z + nz - step) % nz, 0).wait_send()
        for step in range(half - 1):
            along(k, block, (z + step) % nz, 1).wait_send()
    for copy in (own_x, own_y, above):
        copy.wait_send()


def flow_kernel(ga, gb, la, lb, ha, hb, uf_ref, vf_ref, fv_ref, t_ref, s_ref, bnd_ref, uu, vv, pp, cnt, top):
    lev = lax.axis_index("lev")
    sides = (
        ((uu, vv), ((la, 0), (ga, 0), (ga, 512), (ha, 0))),
        ((t_ref, s_ref), ((lb, 128), (gb, 0), (gb, 640), (hb, 0))),
    )
    for fields, sources in sides:
        for part, (ref, base) in enumerate(sources):
            for f, out in enumerate(fields):
                for k in range(2):
                    off = base + f * 256 + k * 128
                    r = part * 4 + k * 2
                    out[r : r + 2] = ref[:, :, off : off + 128].reshape(128, 128).T.reshape(2, 64, 128)
    aux = gb[:, :, 512:640].reshape(128, 128).T
    aux_l = lb[:, :, 0:128].reshape(128, 128).T
    aux_h = hb[:, :, 512:640].reshape(128, 128).T
    cnt[0:4], cnt[4:12], cnt[12:16] = aux_l[4:8], aux[0:8], aux_h[0:4]
    top[0:4], top[4:12], top[12:16] = aux_l[12:16], aux[8:16], aux_h[8:12]

    row, col = iota((64, 64), 0), iota((64, 64), 1)
    down = jnp.where(col < row, 1.0, jnp.where(col == row, 0.5, 0.0)).astype(BF16)
    down = jnp.concatenate([down] * 3, axis=1)
    deep = jnp.where(col >= row, 1.0, 0.0).astype(BF16)
    deep = jnp.concatenate([deep] * 3, axis=1)
    for r in range(16):
        dense = 0.8 * s_ref[r] - 0.2 * t_ref[r]
        total = jnp.dot(down, jnp.concatenate(pieces(dense), axis=0), preferred_element_type=F32)
        pp[r] = buoyancy * (top[r : r + 1] + total)

    level = iota((64, 128), 0).astype(F32)
    uf_ref[0] = jnp.zeros((64, 128), F32)
    vf_ref[0] = jnp.zeros((64, 128), F32)
    for r in (14, 15):
        uf_ref[r] = jnp.zeros((64, 128), F32)
        vf_ref[r] = jnp.zeros((64, 128), F32)
    for r in range(1, 14):
        here, east = cnt[r : r + 1], cnt[r + 1 : r + 2]
        north = pltpu.roll(jnp.broadcast_to(here, (8, 128)), 127, 1)[0:1]
        p, u, v = pp[r], uu[r], vv[r]
        lap_u = uu[r + 1] + uu[r - 1] + pltpu.roll(u, 127, 1) + pltpu.roll(u, 1, 1) - 4.0 * u
        lap_v = vv[r + 1] + vv[r - 1] + pltpu.roll(v, 127, 1) + pltpu.roll(v, 1, 1) - 4.0 * v
        new_u = u + marine_advance * (p - pp[r + 1] + viscosity * lap_u)
        new_v = v + marine_advance * (p - pltpu.roll(p, 127, 1) + viscosity * lap_v)
        uf_ref[r] = jnp.where(level < jnp.minimum(here, east), new_u, 0.0)
        vf_ref[r] = jnp.where(level < jnp.minimum(here, north), new_v, 0.0)

    zero = jnp.zeros((1, 128), F32)
    first = lev == 0
    for r in range(16):
        if 2 <= r < 14:
            u, v = uf_ref[r], vf_ref[r]
            div = u - uf_ref[r - 1] + v - pltpu.roll(v, 1, 1)
            fv = jnp.dot(deep, jnp.concatenate(pieces(div), axis=0), preferred_element_type=F32)
            fv_ref[r] = fv
            flow = fv[0:1]
        else:
            fv_ref[r] = jnp.zeros((64, 128), F32)
            flow = zero
        u2 = jnp.where(first, uf_ref[r, 62:64], uf_ref[r, 0:2])
        v2 = jnp.where(first, vf_ref[r, 62:64], vf_ref[r, 0:2])
        t1 = jnp.where(first, t_ref[r, 63:64], t_ref[r, 0:1])
        s1 = jnp.where(first, s_ref[r, 63:64], s_ref[r, 0:1])
        bnd_ref[r] = jnp.concatenate([u2, v2, flow, t1, s1, zero], axis=0)


def fill_matrix(c_ref, guild_ref, light_ref, w_ref):
    kinds = iota((8, 64), 0) == guild_ref[...]
    light = jnp.sum(jnp.where(iota((8, 8), 0) == iota((8, 8), 1), light_ref[...], 0.0), axis=1, keepdims=True)
    absorb = jnp.sum(jnp.where(kinds, light, 0.0), axis=0, keepdims=True)
    absorb = jnp.broadcast_to(absorb, (8, 64))
    place, across = iota((512, 64), 0), iota((64, 512), 1)
    spread = jnp.where(place // 8 % 16 * 4 + place // 128 == iota((512, 64), 1), 1.0, 0.0).astype(BF16)
    across = jnp.where(across // 8 % 16 * 4 + across // 128 == iota((64, 512), 0), 1.0, 0.0).astype(BF16)
    tall = jnp.dot(spread, c_ref[...], preferred_element_type=F32).astype(BF16)
    wide = jnp.dot(tall, across, preferred_element_type=F32)
    w_ref[0:512] = jnp.where(iota((512, 512), 0) % 8 == iota((512, 512), 1) % 8, wide, 0.0).astype(BF16)
    own = iota((8, 512), 0) == iota((8, 512), 1) % 8
    rows = []
    for part in pieces(absorb):
        line = jnp.dot(part, across, preferred_element_type=F32)
        rows.append(jnp.where(own, line, 0.0))
    rows.append(jnp.zeros((8, 512), F32))
    w_ref[512:544] = jnp.concatenate(rows, axis=0).astype(BF16)


def react_kernel(
    nz, uf_ref, vf_ref, fv_ref, t_ref, s_ref, edge_ref, se_ref, c_ref, guild_ref, light_ref,
    adv_ref, back_ref, scale_ref, att_ref, attp_ref, oc_ref, adv_out, att_out, oc_out, out_sems,
    up, um, vp, vm, fp, fm, q1, ex, tr, yd, vpt, vmt, vpu, vmu, rest, bnd_ref, w_ref, send_ref, got, res, sizes,
    s1, r1, s2, r2, s3, r3, s4, r4,
):
    z, lev = lax.axis_index("trc"), lax.axis_index("lev")
    first = lev == 0
    sub = iota((8, 128), 0)
    peer = {"lev": 1 - lev}
    def rdma(src, dst, send, recv, to):
        return pltpu.make_async_remote_copy(
            src_ref=src, dst_ref=dst, send_sem=send, recv_sem=recv, device_id=to, device_id_type=MESH
        )

    def each(body):
        def one(i, carry):
            d = nz // 2 + (i + 1) // 2 * (1 - i % 2 * 2)
            body((z + d) % nz)
            return carry

        lax.fori_loop(0, nz - 1, one, 0)

    def out(t, to, at):
        return rdma(send_ref.at[t, to], got.at[t, at], s1.at[t, to], r1.at[t, at], {"trc": to})

    def home(c, to, at):
        return rdma(res.at[c, :, to], back_ref.at[c, :, at], s2.at[c, to], r2.at[c, at], {"trc": to})

    def size(c, to, at):
        return rdma(sizes.at[c, to], scale_ref.at[c, at], s4.at[c, to], r4.at[c, at], {"trc": to})

    def stored(t):
        return pltpu.make_async_copy(adv_ref.at[t], adv_out.at[t], out_sems.at[t])

    def own_back(c):
        return pltpu.make_async_copy(res.at[c, :, z], back_ref.at[c, :, z], out_sems.at[4 + c])

    def own_scale(c):
        return pltpu.make_async_copy(sizes.at[c, z], scale_ref.at[c, z], out_sems.at[8 + c])

    ocean = pltpu.make_async_copy(oc_ref, oc_out, out_sems.at[12])
    shades = pltpu.make_async_copy(att_ref, att_out, out_sems.at[13])
    edges = rdma(edge_ref.at[1:14], bnd_ref.at[1:14], s3.at[0], r3.at[0], peer)
    edges.start()
    mine = pl.multiple_of(z * 8, 8)
    for f, ref in enumerate((uf_ref, vf_ref)):
        for k in range(4):
            tr[...] = ref[4 + 2 * k : 6 + 2 * k].reshape(128, 128).T
            oc_ref[2 + f, :, k * 128 : k * 128 + 128] = tr[pl.ds(mine, 8), :]
    fill_matrix(c_ref, guild_ref, light_ref, w_ref)
    bnd_ref[0] = jnp.zeros((8, 128), F32)
    edges.wait_recv()

    def rows(r):
        return pl.ds(pl.multiple_of(r * 80, 8), 80)

    def around(own, above, below):
        return jnp.concatenate(
            [jnp.where(first, 0.0, above), own, jnp.where(first, below, 0.0)], axis=0
        )

    def faces(r, carry):
        edge = bnd_ref[r]
        edge_w = bnd_ref[r - 1]
        pos = pltpu.roll(edge, 6, 0)
        u_ext = around(uf_ref[r], jnp.where(sub >= 6, pos, 0.0), jnp.where(sub < 2, edge, 0.0))
        two = pltpu.roll(edge, 4, 0)
        low = pltpu.roll(edge, 6, 0)
        v_ext = around(vf_ref[r], jnp.where(sub >= 6, two, 0.0), jnp.where(sub < 2, low, 0.0))
        d2 = edge[0:2] - edge_w[0:2] + edge[2:4] - pltpu.roll(edge, 1, 1)[2:4]
        d0, d1 = d2[0:1], d2[1:2]
        flow = jnp.where(first, edge[4:5], 0.0)
        f_own = fv_ref[r] + flow
        above = jnp.where(sub == 7, f_own[0:1] + d1, jnp.where(sub == 6, f_own[0:1] + d1 + d0, 0.0))
        below = jnp.where(
            sub == 0, flow, jnp.where(sub == 1, flow - d0, jnp.where(sub == 2, flow - d0 - d1, 0.0))
        )
        surface = jnp.where((iota((64, 128), 0) == 0) & first, 0.0, f_own)
        f_ext = level_step * around(surface, above, below)
        u_ext = tracer_step * u_ext
        v_ext = tracer_step * v_ext
        up[r], um[r] = jnp.maximum(u_ext, 0.0), jnp.minimum(u_ext, 0.0)
        vp[rows(r)], vm[rows(r)] = jnp.maximum(v_ext, 0.0), jnp.minimum(v_ext, 0.0)
        fp[r], fm[r] = jnp.maximum(f_ext, 0.0), jnp.minimum(f_ext, 0.0)
        return carry

    lax.fori_loop(1, 14, faces, 0)

    def turn_faces(ref, wide, narrow):
        for c in range(9):
            wide[c] = ref[64 + 128 * c : 192 + 128 * c].T
        for k in range(4):
            row = (4 + 2 * k) * 80 + 8
            both = jnp.concatenate([ref[row : row + 64], ref[row + 80 : row + 144]], axis=0)
            narrow[k] = both.T

    turn_faces(vp, vpt, vpu)
    turn_faces(vm, vmt, vmu)

    def along_y(q, plus, minus):
        north = 0.5 * (pltpu.roll(q, 127, 0) - q)
        slope = minmod_half(pltpu.roll(north, 1, 0), north)
        flux = plus * (q + slope) + minus * pltpu.roll(q - slope, 127, 0)
        return flux - pltpu.roll(flux, 1, 0)

    def sweep(load, store, start, stop):
        d_a = 0.5 * (load(start - 1) - load(start - 2))
        d_b = 0.5 * (load(start) - load(start - 1))
        d_c = 0.5 * (load(start + 1) - load(start))
        right = load(start - 1) + minmod_half(d_a, d_b)
        slope = minmod_half(d_b, d_c)
        flux = up[start - 1] * right + um[start - 1] * (load(start) - slope)

        def one(r, carry):
            d_here, right, flux = carry
            q, q_e = load(r), load(r + 1)
            d_next = 0.5 * (load(r + 2) - q_e)
            slope = minmod_half(d_here, d_next)
            flux_e = up[r] * right + um[r] * (q_e - slope)
            change = flux_e - flux
            right_e = q_e + slope
            below = 0.5 * (pltpu.roll(q, 79, 0) - q)
            slope = minmod_half(pltpu.roll(below, 1, 0), below)
            flux_v = fp[r] * pltpu.roll(q + slope, 1, 0) + fm[r] * (q - slope)
            change = change + (pltpu.roll(flux_v, 79, 0) - flux_v)
            store(r, q - change)
            return d_next, right_e, flux_e

        lax.fori_loop(start, stop, one, (d_c, load(start) + slope, flux))

    def tracer(t, carry):
        def first_load(r):
            return se_ref[t, r]

        def first_store(r, value):
            q1[rows(r)] = value - yd[rows(r)]

        def second_load(r):
            return q1[rows(r)]

        def second_store(r, value):
            rest[r - 4] = value[8:72]

        for c in range(9):
            start, stop = 64 + 128 * c, 192 + 128 * c
            q = [se_ref[t, r, max(start - r * 80, 0) : min(stop - r * 80, 80)] for r in range(start // 80, (stop + 79) // 80)]
            q = jnp.concatenate(q, axis=0).T
            yd[64 + 128 * c : 192 + 128 * c] = along_y(q, vpt[c], vmt[c]).T
        sweep(first_load, first_store, 2, 14)
        sweep(second_load, second_store, 4, 12)
        for k in range(4):
            row = (4 + 2 * k) * 80 + 8
            q = jnp.concatenate([q1[row : row + 64], q1[row + 80 : row + 144]], axis=0).T
            new = rest[2 * k : 2 * k + 2].reshape(128, 128).T - along_y(q, vpu[k], vmu[k])
            adv_ref[t, k] = new
            send_ref[t, :, :, k * 128 : k * 128 + 128] = new.reshape(16, 8, 128).astype(BF16)
        each(lambda to: out(t, to, z).start())
        got[t, z] = send_ref[t, z]
        stored(t).start()
        return carry

    lax.fori_loop(0, 4, tracer, 0)

    for f, ref in enumerate((t_ref, s_ref)):
        for r in range(3, 13):
            edge = bnd_ref[r][5 + f : 6 + f]
            ex[r] = around(ref[r], jnp.where(sub == 7, edge, 0.0), jnp.where(sub == 0, edge, 0.0))

        def donor(r, flux_w):
            c = ex[r]
            flux = up[r] * c + um[r] * ex[r + 1]
            flux_n = vp[rows(r)] * c + vm[rows(r)] * pltpu.roll(c, 127, 1)
            flux_v = fp[r] * pltpu.roll(c, 1, 0) + fm[r] * c
            wide = flux - flux_w + (flux_n - pltpu.roll(flux_n, 1, 1))
            tall = pltpu.roll(flux_v, 79, 0) - flux_v
            new = c - (marine_advance / tracer_step) * wide - (marine_advance / level_step) * tall
            q1[rows(r)] = new
            return flux

        lax.fori_loop(4, 12, donor, up[3] * ex[3] + um[3] * ex[4])
        for k in range(4):
            row = (4 + 2 * k) * 80 + 8
            both = jnp.concatenate([q1[row : row + 64], q1[row + 80 : row + 144]], axis=0)
            tr[...] = both.T
            oc_ref[f, :, k * 128 : k * 128 + 128] = tr[pl.ds(mine, 8), :]
    ocean.start()

    lax.fori_loop(0, 4, lambda t, carry: (each(lambda at: out(t, at, at).wait_recv()), carry)[1], 0)
    for c in range(4):
        values = got[:, :, :, c * 128 : c * 128 + 128].reshape(512, 128)
        values = jnp.dot(w_ref[...], values, preferred_element_type=F32)
        att_ref[c] = values[512:520] + values[520:528] + values[528:536]
        values = values[0:512].reshape(4, nz, 8, 128)
        largest = jnp.max(jnp.max(jnp.abs(values), axis=0), axis=1, keepdims=True)
        largest = jnp.maximum(largest, 1e-30)
        sizes[c] = largest * (1.0 / 32767.0)
        coded = jnp.round(values * (32767.0 / largest)[None])
        res[c] = coded.astype(jnp.int32).astype(I16)
        each(lambda to: (home(c, to, z).start(), size(c, to, z).start()))
        own_back(c).start()
        own_scale(c).start()
    shade = rdma(att_ref, attp_ref, s3.at[1], r3.at[1], peer)
    shade.start()
    shades.start()
    for c in range(4):

        def finish(at):
            home(c, at, at).wait_recv()
            size(c, at, at).wait_recv()
            out(c, at, at).wait_send()
            home(c, at, at).wait_send()
            size(c, at, at).wait_send()

        each(finish)
    shade.wait_recv()
    shade.wait_send()
    edges.wait_send()
    for c in range(4):
        stored(c).wait()
        own_back(c).wait()
        own_scale(c).wait()
    ocean.wait()
    shades.wait()


GATHERED = 7
LOADED = 10
ARRIVALS = 9
FLOWS = 6


def step_kernel(nz, nx, *refs):
    fields, params, outs, scratch = refs[:6], refs[6:9], refs[9:15], refs[15:]
    gathered, scratch = scratch[:GATHERED], scratch[GATHERED:]
    loaded, scratch = scratch[: LOADED + ARRIVALS], scratch[LOADED + ARRIVALS :]
    flows, scratch = scratch[:FLOWS], scratch[FLOWS:]
    temporary, scratch = scratch[:5], scratch[5:]
    held, scratch = scratch[:3], scratch[3:]
    param_sems, out_sems, adv_ref, att_ref, oc_ref = scratch[:5]
    loads = [pltpu.make_async_copy(src, dst, param_sems.at[i]) for i, (src, dst) in enumerate(zip(params, held))]
    for load in loads:
        load.start()
    gather_kernel(nz, nx, *fields, *gathered, *loaded)
    flow_kernel(*gathered[:6], *flows, *temporary)
    for load in loads:
        load.wait()
    adv_out, back_ref, scale_ref, att_out, attp_ref, oc_out = outs
    react_kernel(
        nz, *flows, gathered[6], *held, adv_ref, back_ref, scale_ref, att_ref, attp_ref, oc_ref,
        adv_out, att_out, oc_out, out_sems, *scratch[5:]
    )


def final_kernel(
    adv_hbm, back_hbm, scale_hbm, att_hbm, attp_hbm, oc_hbm, m_hbm,
    w_hbm, s_hbm, u_hbm, v_hbm, sp_hbm,
    adv_ref, back_ref, scale_ref, att_ref, attp_ref, oc_ref, m_ref, w_ref, s_ref, u_ref, v_ref, sp_ref,
    ins, outs,
):
    lev = lax.axis_index("lev")
    smalls = [
        pltpu.make_async_copy(src, dst, ins.at[i])
        for i, (src, dst) in enumerate(
            ((scale_hbm, scale_ref), (att_hbm, att_ref), (attp_hbm, attp_ref), (oc_hbm, oc_ref), (m_hbm, m_ref))
        )
    ]
    backs = [pltpu.make_async_copy(back_hbm.at[:, t], back_ref.at[:, t], ins.at[5 + t]) for t in range(4)]
    advs = [pltpu.make_async_copy(adv_hbm.at[t], adv_ref.at[t], ins.at[9 + t]) for t in range(4)]
    for copy in smalls:
        copy.start()
    for t in range(4):
        backs[t].start()
        advs[t].start()
    for copy in smalls:
        copy.wait()
    row, col = iota((128, 128), 0), iota((128, 128), 1)
    same = row // 64 == col // 64
    before = jnp.where(same & (row < col), 1.0, 0.0).astype(BF16)
    every = jnp.where(same & (lev == 1), 1.0, 0.0).astype(BF16)
    sums = jnp.concatenate([before] * 3 + [every] * 3, axis=0)
    for c in range(4):
        att = att_ref[c]
        terms = jnp.concatenate(pieces(att) + pieces(attp_ref[c]), axis=1)
        path = jnp.dot(terms, sums, preferred_element_type=F32)
        caught = jnp.exp(-path) * (1.0 - jnp.exp(-att))
        wet = jnp.concatenate([m_ref[2 * c], m_ref[2 * c + 1]], axis=1).astype(F32)
        lanes = slice(c * 128, c * 128 + 128)
        warm = oc_ref[0, :, lanes] + warming_amount * wet * caught
        for out, value in ((w_ref, warm), (s_ref, oc_ref[1, :, lanes]), (u_ref, oc_ref[2, :, lanes]), (v_ref, oc_ref[3, :, lanes])):
            out[2 * c] = value[:, 0:64]
            out[2 * c + 1] = value[:, 64:128]
    done = [
        pltpu.make_async_copy(src, dst, outs.at[i])
        for i, (src, dst) in enumerate(((w_ref, w_hbm), (s_ref, s_hbm), (u_ref, u_hbm), (v_ref, v_hbm)))
    ]
    for copy in done:
        copy.start()
    for t in range(4):
        backs[t].wait()
        advs[t].wait()
        for c in range(4):
            react = back_ref[c, t].astype(jnp.int32).astype(F32) * scale_ref[c]
            new = (adv_ref[t, c] + react_step * react.reshape(128, 128)).T
            sp_ref[t, pl.ds(2 * c, 64, stride=8), :] = new[0:64]
            sp_ref[t, pl.ds(2 * c + 1, 64, stride=8), :] = new[64:128]
        done.append(pltpu.make_async_copy(sp_ref.at[t], sp_hbm.at[t], outs.at[4 + t]))
        done[-1].start()
    for copy in done:
        copy.wait()


def shards(
    nz,
    nx,
    potential_warmth,
    saltiness_anomaly,
    zonal_speed,
    meridional_speed,
    marine_indicator,
    species_concentrations,
    coupling_matrix,
    species_guild_number,
    guild_extinction_coefficient,
):
    tiles = [
        jnp.transpose(a, (1, 2, 0))
        for a in (potential_warmth, saltiness_anomaly, zonal_speed, meridional_speed, marine_indicator)
    ]
    species = species_concentrations.reshape(4, 512, 128)
    dma = pltpu.SemaphoreType.DMA
    tile = pltpu.VMEM((8, 8, 64), F32)
    row, column = pltpu.VMEM((16, 64, 128), F32), pltpu.VMEM((16, 128), F32)
    tall, flat = pltpu.VMEM((16, 80, 128), F32), pltpu.VMEM((1280, 128), F32)
    edge = pltpu.VMEM((16, 8, 128), F32)
    adv, back, scale, att, attp, ocean = pl.pallas_call(
        functools.partial(step_kernel, nz, nx),
        out_shape=(
            sds((4, 4, 128, 128)),
            sds((4, 4, nz, 8, 128), I16),
            sds((4, nz, 1, 128)),
            sds((4, 8, 128)),
            sds((4, 8, 128)),
            sds((4, 8, 512)),
        ),
        in_specs=[pl.BlockSpec(memory_space=pltpu.HBM)] * 9,
        out_specs=(pl.BlockSpec(memory_space=pltpu.HBM),) * 6,
        scratch_shapes=[pltpu.VMEM((nz, 8, lanes), F32) for lanes in (SPEEDS, WATER, 512, 640, 512, 640)]
        + [pltpu.VMEM((4, 16, 80, 128), F32)]
        + [tile] * 4
        + [
            pltpu.VMEM((8, 8, 64), jnp.int32),
            pltpu.VMEM((4, 512, 128), F32),
            pltpu.VMEM((8, SPEEDS), F32),
            pltpu.VMEM((8, WATER), F32),
            pltpu.VMEM((8, 128), F32),
            pltpu.VMEM((8, 128), F32),
            dma((6,)),
            dma((2, 2, nz)),
        ]
        + [dma((2, nz))] * 5
        + [dma((6,))] * 2
        + [row] * 5
        + [edge, row, row, row, column, column]
        + [
            pltpu.VMEM((64, 64), BF16),
            pltpu.VMEM((1, 64), jnp.int32),
            pltpu.VMEM((1, 8), F32),
            dma((3,)),
            dma((14,)),
            pltpu.VMEM((4, 4, 128, 128), F32),
            pltpu.VMEM((4, 8, 128), F32),
            pltpu.VMEM((4, 8, 512), F32),
        ]
        + [tall, tall, flat, flat, tall, tall, flat, tall]
        + [
            pltpu.VMEM((128, 128), F32),
            flat,
            pltpu.VMEM((9, 128, 128), F32),
            pltpu.VMEM((9, 128, 128), F32),
            pltpu.VMEM((4, 128, 128), F32),
            pltpu.VMEM((4, 128, 128), F32),
            pltpu.VMEM((8, 64, 128), F32),
            edge,
            pltpu.VMEM((544, 512), BF16),
            pltpu.VMEM((4, nz, 8, 512), BF16),
            pltpu.VMEM((4, nz, 8, 512), BF16),
            pltpu.VMEM((4, 4, nz, 8, 128), I16),
            pltpu.VMEM((4, nz, 1, 128), F32),
        ]
        + [dma((4, nz))] * 4
        + [dma((2,))] * 2
        + [dma((4, nz))] * 2,
        compiler_params=pltpu.CompilerParams(collective_id=0, has_side_effects=True, vmem_limit_bytes=60 << 20),
        name="step",
    )(
        *tiles, species, coupling_matrix,
        species_guild_number.reshape(1, 64), guild_extinction_coefficient.reshape(1, 8),
    )

    hbm = pl.BlockSpec(memory_space=pltpu.HBM)
    warm, salt, zonal, merid, final = pl.pallas_call(
        final_kernel,
        out_shape=(sds((8, 8, 64)),) * 4 + (sds((4, 512, 128)),),
        in_specs=[hbm] * 7,
        out_specs=(hbm,) * 5,
        scratch_shapes=[
            pltpu.VMEM((4, 4, 128, 128), F32),
            pltpu.VMEM((4, 4, nz, 8, 128), I16),
            pltpu.VMEM((4, nz, 1, 128), F32),
            pltpu.VMEM((4, 8, 128), F32),
            pltpu.VMEM((4, 8, 128), F32),
            pltpu.VMEM((4, 8, 512), F32),
            pltpu.VMEM((8, 8, 64), jnp.int32),
        ]
        + [tile] * 4
        + [pltpu.VMEM((4, 512, 128), F32), dma((13,)), dma((8,))],
        compiler_params=pltpu.CompilerParams(vmem_limit_bytes=60 << 20),
        name="final",
    )(adv, back, scale, att, attp, ocean, tiles[4])
    warm, salt, zonal, merid = (jnp.transpose(a, (2, 0, 1)) for a in (warm, salt, zonal, merid))
    return warm, salt, zonal, merid, final.reshape(4, 64, 8, 128)


def solution(mesh):
    tile, tracers = P("lev", "cols", "trc"), P("trc", "lev", "cols", None)
    return jax.shard_map(
        functools.partial(shards, mesh.shape["trc"], mesh.shape["cols"]),
        mesh=mesh,
        in_specs=(tile, tile, tile, tile, tile, tracers, P(), P(), P()),
        out_specs=(tile, tile, tile, tile, tracers),
        check_vma=False,
    )
```

time: 144 us -> 118 us (0.82)
  Pallas kernels: 127 us -> 116 us
  local copies, waits for them, and re-layouts: 7.39 us -> 0 us
  starting transfers between devices: 5.62 us -> 0 us
  other arithmetic: 1.62 us -> 0 us
    pallas_call x6 -> x2, Pallas kernels: 127 us -> 116 us  [the longest x1 113 us: shards(): pl.pallas_call(functools.partial(step_kernel, nz, nx), out_shape=(sds((4,...]
    unnamed x18 -> x0, local copies, waits for them, and re-layouts: 7.24 us -> none
    ppermute x1 -> x0, starting transfers between devices: 5.62 us -> none  [shards(): above = lax.ppermute(dense, 'lev', [(0, 1)])]
    reduce_sum x2 -> x0, other arithmetic: 1.62 us -> none  [the longest x1 0.86 us: shards(): dense = jnp.sum(0.8 * tiles[1] - 0.2 * tiles[0], axis=2)]
  transfers between devices with their start and end apart: 1 -> 0, of which waited for: 0 -> 0; matrix products, arithmetic and copies ran while one was open for 1% -> 0% of each run, Pallas kernels for 0% -> 0%
where the time goes in v3:
time: 118 us; the launch traced here: 117 us
  Pallas kernels  116 us (98%)
    pallas_call x1, Pallas kernels, shards(): pl.pallas_call(functools.partial(step_kernel, nz, nx), out_shape=(sds((4,...  113 us
    pallas_call x1, Pallas kernels, shards(): pl.pallas_call(final_kernel, out_shape=(sds((8, 8, 64)),) * 4 + (sds((4,...  2.66 us

profile of v3, /device:TPU:1, one launch (start us, length us, event | category | flops | bytes accessed | tf_op | source)
XLA Modules:
  0.0 116.7 jit_solution(10806711300124622914)
XLA Ops:
  0.6 113.4 %step.1 = (f32[4,4,128,128]{3,2,1,0:T(8,128)}, s16[4,4,16,8,128]{4,3,2,1,0:T(8,128)(2,1)}, f32[4,16,1,128]{3,2,1,0:T(1,128)}, f32[4,8,128]{2,1,0:T(8,128)}, f32[4,8,128]{2,1,0:T(8,128)}, /*index=5*/f32[4,8,512]{2,1,0:T(8,128)}) custom-call(f32[8,8,64]{2,1,0:T(8,128)} %bitcast.16, f32[8,8,64]{2,1,0:T(8,128)} %bitcast.17, f32[8,8,64]{2,1,0:T(8,128)} %bitcast.18, ...), custom_call_target="tpu_custom_call" | custom-call | tf_op jit(solution)/shard_map/step/pallas_call | solution.py:613
  114.0 2.7 %final.1 = (f32[8,8,64]{2,1,0:T(8,128)}, f32[8,8,64]{2,1,0:T(8,128)}, f32[8,8,64]{2,1,0:T(8,128)}, f32[8,8,64]{2,1,0:T(8,128)}, f32[4,512,128]{2,1,0:T(8,128)}) custom-call(f32[4,4,128,128]{3,2,1,0:T(8,128)} %get-tuple-element.16.adv_hbm, s16[4,4,16,8,128]{4,3,2,1,0:T(8,128)(2,1)} %get-tuple-element.17.back_hbm, ...), custom_call_target="tpu_custom_call" | custom-call | tf_op jit(solution)/shard_map/final/pallas_call | solution.py:679

commit v4 on v3

--- a/solution.py
+++ b/solution.py
@@ -20,7 +20,7 @@
 react_step = 0.25
 warming_amount = 60.0
 
-SPEEDS, WATER = 1024, 1152
+SPEEDS, DENSITY, WATER = 1024, 640, 1024
 
 
 def sds(shape, dtype=F32):
@@ -45,9 +45,9 @@
 
 def gather_kernel(
     nz, nx, t_hbm, s_hbm, u_hbm, v_hbm, m_hbm, sp_hbm,
-    ga, gb, la, lb, ha, hb, se,
-    t_in, s_in, u_in, v_in, m_in, sp_in, a_own, b_own, d_own, d_peer,
-    ins, zs, zr, ls, lr, hs, hr, ss, sr,
+    ga, gb, gt, la, lb, lt, ha, hb, ht, se,
+    t_in, s_in, u_in, v_in, m_in, sp_in, a_own, b_own, t_own, d_own, d_peer,
+    ins, zs, zr, ls, lr, hs, hr, ss, sr, ts, tr,
 ):
     z, x, lev = lax.axis_index("trc"), lax.axis_index("cols"), lax.axis_index("lev")
     zup, zdn = {"trc": (z + 1) % nz}, {"trc": (z + nz - 1) % nz}
@@ -61,15 +61,12 @@
     ]
     for load in loads:
         load.start()
+    for ref in (gt, lt, ht):
+        ref[...] = jnp.zeros_like(ref)
     barrier = pltpu.get_barrier_semaphore()
-    for other in (xup, xdn, peer):
+    two_up, two_dn = {"trc": (z + 2) % nz}, {"trc": (z + nz - 2) % nz}
+    for other in (zup, zdn, two_up, two_dn, xup, xdn, peer):
         pl.semaphore_signal(barrier, inc=1, device_id=other, device_id_type=MESH)
-
-    def greet(d, carry):
-        pl.semaphore_signal(barrier, inc=1, device_id={"trc": (z + d) % nz}, device_id_type=MESH)
-        return carry
-
-    lax.fori_loop(1, nz, greet, 0)
 
     def rdma(src, dst, send, recv, to):
         return pltpu.make_async_remote_copy(
@@ -77,16 +74,17 @@
         )
 
     wholes, lefts, rights = (ga, gb), (la, lb), (ha, hb)
-    upper, lower = (SPEEDS // 2, 512), (SPEEDS // 2, 640)
-
-    def along(k, src, source, way):
-        return rdma(src, wholes[k].at[source], zs.at[k, way, source], zr.at[k, source], zup if way == 0 else zdn)
+    upper, lower = (512, 256), (512, 384)
+
+    def along(k, src, source, way, hop):
+        to = {"trc": (z + (hop if way == 0 else nz - hop)) % nz}
+        return rdma(src, wholes[k].at[source], zs.at[k], zr.at[k, source], to)
 
     def to_right(k, src, source):
-        return rdma(src.at[:, upper[k] :], lefts[k].at[source], ls.at[k, source], lr.at[k, source], xup)
+        return rdma(src.at[:, upper[k] :], lefts[k].at[source], ls.at[k], lr.at[k], xup)
 
     def to_left(k, src, source):
-        return rdma(src.at[:, : lower[k]], rights[k].at[source], hs.at[k, source], hr.at[k, source], xdn)
+        return rdma(src.at[:, : lower[k]], rights[k].at[source], hs.at[k], hr.at[k], xdn)
 
     def fill(block, refs, high):
         for f, ref in enumerate(refs):
@@ -95,8 +93,9 @@
                 block[:, off : off + 128] = jnp.concatenate([ref[2 * k], ref[2 * k + 1]], axis=1)
 
     def begin(k, block):
-        along(k, block, z, 0).start()
-        along(k, block, z, 1).start()
+        for hop in (2, 1):
+            along(k, block, z, 0, hop).start()
+            along(k, block, z, 1, hop).start()
         to_right(k, block, z).start()
         to_left(k, block, z).start()
         wholes[k][z] = block[...]
@@ -104,22 +103,25 @@
     loads[0].wait()
     loads[1].wait()
     fill(a_own, (u_in, v_in), 512)
-    pl.semaphore_wait(barrier, nz + 2)
+    pl.semaphore_wait(barrier, 7)
     begin(0, a_own)
 
     for load in loads[2:5]:
         load.wait()
+    rho = u_in
     lane = iota((8, 128), 1)
     counts = jnp.zeros((8, 128), F32)
     dense = jnp.zeros((8, 128), F32)
     for i in range(8):
         counts = counts + jnp.where(lane == i, jnp.sum(m_in[i].astype(F32), axis=1, keepdims=True), 0.0)
-        column = jnp.sum(0.8 * s_in[i] - 0.2 * t_in[i], axis=1, keepdims=True)
+        rho[i] = 0.8 * s_in[i] - 0.2 * t_in[i]
+        column = jnp.sum(rho[i], axis=1, keepdims=True)
         dense = dense + jnp.where(lane == i + 8, column, 0.0)
     d_own[...] = dense
     above = rdma(d_own, d_peer, ss.at[5], sr.at[5], peer)
     above.start()
-    fill(b_own, (t_in, s_in), 640)
+    fill(b_own, (rho,), 384)
+    fill(t_own, (t_in, s_in), 512)
 
     loads[5].wait()
 
@@ -138,8 +140,17 @@
         for i, low, high in ((2, 4, 12), (3, 0, 4), (4, 12, 16))
     ]
     above.wait_recv()
-    b_own[:, 512:640] = counts + jnp.where(lev == 1, d_peer[...], 0.0)
+    b_own[:, 256:384] = counts + jnp.where(lev == 1, d_peer[...], 0.0)
     begin(1, b_own)
+    near_water = [
+        rdma(t_own, gt.at[z], ts.at[0], tr.at[0], zup),
+        rdma(t_own, gt.at[z], ts.at[1], tr.at[1], zdn),
+        rdma(t_own.at[:, 512:], lt.at[z], ts.at[2], tr.at[2], xup),
+        rdma(t_own.at[:, :512], ht.at[z], ts.at[3], tr.at[3], xdn),
+    ]
+    for copy in near_water:
+        copy.start()
+    gt[z] = t_own[...]
     own_x.start()
     own_y.start()
     parts[0].start()
@@ -155,9 +166,11 @@
         for k in range(2):
             for way, source in ((0, (z + nz - step) % nz), (1, (z + step) % nz))[: 2 if step < half else 1]:
                 block = wholes[k].at[source]
-                along(k, block, source, way).wait_recv()
-                if step < half - way:
-                    along(k, block, source, way).start()
+                along(k, block, source, way, 1).wait_recv()
+                if step % 2 == 0:
+                    for hop in (2, 1):
+                        if step + hop <= half - way:
+                            along(k, block, source, way, hop).start()
                 came.append((k, block, source))
         for k, block, source in came:
             to_right(k, block, source).start()
@@ -172,29 +185,26 @@
         part.wait_recv()
         part.wait_send()
 
-    for k, block in ((0, a_own), (1, b_own)):
-
-        def arrived(source, carry):
-            to_right(k, block, source).wait_recv()
-            to_left(k, block, source).wait_recv()
-            to_right(k, block, source).wait_send()
-            to_left(k, block, source).wait_send()
-            return carry
-
-        lax.fori_loop(0, nz, arrived, 0)
-        for step in range(half):
-            along(k, block, (z + nz - step) % nz, 0).wait_send()
-        for step in range(half - 1):
-            along(k, block, (z + step) % nz, 1).wait_send()
+    for k in range(2):
+        for ref, send, recv in ((lefts[k], ls, lr), (rights[k], hs, hr)):
+            copies = rdma(ref, ref, send.at[k], recv.at[k], xup)
+            copies.wait_recv()
+            copies.wait_send()
+        blocks = wholes[k].at[0 : nz - 1]
+        rdma(blocks, blocks, zs.at[k], zr.at[k, z], zup).wait_send()
+    for copy in near_water:
+        copy.wait_recv()
+        copy.wait_send()
     for copy in (own_x, own_y, above):
         copy.wait_send()
 
 
-def flow_kernel(ga, gb, la, lb, ha, hb, uf_ref, vf_ref, fv_ref, t_ref, s_ref, bnd_ref, uu, vv, pp, cnt, top):
+def flow_kernel(ga, gb, gt, la, lb, lt, ha, hb, ht, uf_ref, vf_ref, fv_ref, t_ref, s_ref, bnd_ref, uu, vv, rho, pp, cnt, top):
     lev = lax.axis_index("lev")
     sides = (
         ((uu, vv), ((la, 0), (ga, 0), (ga, 512), (ha, 0))),
-        ((t_ref, s_ref), ((lb, 128), (gb, 0), (gb, 640), (hb, 0))),
+        ((t_ref, s_ref), ((lt, 0), (gt, 0), (gt, 512), (ht, 0))),
+        ((rho,), ((lb, 128), (gb, 0), (gb, 384), (hb, 0))),
     )
     for fields, sources in sides:
         for part, (ref, base) in enumerate(sources):
@@ -203,9 +213,9 @@
                     off = base + f * 256 + k * 128
                     r = part * 4 + k * 2
                     out[r : r + 2] = ref[:, :, off : off + 128].reshape(128, 128).T.reshape(2, 64, 128)
-    aux = gb[:, :, 512:640].reshape(128, 128).T
+    aux = gb[:, :, 256:384].reshape(128, 128).T
     aux_l = lb[:, :, 0:128].reshape(128, 128).T
-    aux_h = hb[:, :, 512:640].reshape(128, 128).T
+    aux_h = hb[:, :, 256:384].reshape(128, 128).T
     cnt[0:4], cnt[4:12], cnt[12:16] = aux_l[4:8], aux[0:8], aux_h[0:4]
     top[0:4], top[4:12], top[12:16] = aux_l[12:16], aux[8:16], aux_h[8:12]
 
@@ -215,8 +225,7 @@
     deep = jnp.where(col >= row, 1.0, 0.0).astype(BF16)
     deep = jnp.concatenate([deep] * 3, axis=1)
     for r in range(16):
-        dense = 0.8 * s_ref[r] - 0.2 * t_ref[r]
-        total = jnp.dot(down, jnp.concatenate(pieces(dense), axis=0), preferred_element_type=F32)
+        total = jnp.dot(down, jnp.concatenate(pieces(rho[r]), axis=0), preferred_element_type=F32)
         pp[r] = buoyancy * (top[r : r + 1] + total)
 
     level = iota((64, 128), 0).astype(F32)
@@ -279,7 +288,7 @@
     nz, uf_ref, vf_ref, fv_ref, t_ref, s_ref, edge_ref, se_ref, c_ref, guild_ref, light_ref,
     adv_ref, back_ref, scale_ref, att_ref, attp_ref, oc_ref, adv_out, att_out, oc_out, out_sems,
     up, um, vp, vm, fp, fm, q1, ex, tr, yd, vpt, vmt, vpu, vmu, rest, bnd_ref, w_ref, send_ref, got, res, sizes,
-    s1, r1, s2, r2, s3, r3, s4, r4,
+    s1, r1, s2, r2, s3, r3, s4, r4, s5, r5,
 ):
     z, lev = lax.axis_index("trc"), lax.axis_index("lev")
     first = lev == 0
@@ -298,14 +307,24 @@
 
         lax.fori_loop(0, nz - 1, one, 0)
 
+    others = pl.ds(0, nz - 1)
+
+    def to_device(to):
+        return peer if to is others else {"trc": to}
+
     def out(t, to, at):
-        return rdma(send_ref.at[t, to], got.at[t, at], s1.at[t, to], r1.at[t, at], {"trc": to})
+        return rdma(send_ref.at[t, to], got.at[t, at], s1.at[t], r1.at[t], to_device(to))
+
+    def last(c, to, at):
+        lanes = slice(c * 128, c * 128 + 128)
+        return rdma(send_ref.at[3, to, :, lanes], got.at[3, at, :, lanes], s5.at[c], r5.at[c], to_device(to))
 
     def home(c, to, at):
-        return rdma(res.at[c, :, to], back_ref.at[c, :, at], s2.at[c, to], r2.at[c, at], {"trc": to})
+        return rdma(res.at[c, :, to], back_ref.at[c, :, at], s2.at[c], r2.at[c], to_device(to))
 
     def size(c, to, at):
-        return rdma(sizes.at[c, to], scale_ref.at[c, at], s4.at[c, to], r4.at[c, at], {"trc": to})
+        return rdma(sizes.at[c, to], scale_ref.at[c, at], s4.at[c], r4.at[c], to_device(to))
+
 
     def stored(t):
         return pltpu.make_async_copy(adv_ref.at[t], adv_out.at[t], out_sems.at[t])
@@ -432,12 +451,18 @@
             new = rest[2 * k : 2 * k + 2].reshape(128, 128).T - along_y(q, vpu[k], vmu[k])
             adv_ref[t, k] = new
             send_ref[t, :, :, k * 128 : k * 128 + 128] = new.reshape(16, 8, 128).astype(BF16)
-        each(lambda to: out(t, to, z).start())
+
+        @pl.when(t < 3)
+        def _():
+            each(lambda to: out(t, to, z).start())
+
         got[t, z] = send_ref[t, z]
         stored(t).start()
         return carry
 
     lax.fori_loop(0, 4, tracer, 0)
+    for c in range(4):
+        each(lambda to: last(c, to, z).start())
 
     for f, ref in enumerate((t_ref, s_ref)):
         for r in range(3, 13):
@@ -463,8 +488,10 @@
             oc_ref[f, :, k * 128 : k * 128 + 128] = tr[pl.ds(mine, 8), :]
     ocean.start()
 
-    lax.fori_loop(0, 4, lambda t, carry: (each(lambda at: out(t, at, at).wait_recv()), carry)[1], 0)
+    for t in range(3):
+        out(t, others, others).wait_recv()
     for c in range(4):
+        last(c, others, others).wait_recv()
         values = got[:, :, :, c * 128 : c * 128 + 128].reshape(512, 128)
         values = jnp.dot(w_ref[...], values, preferred_element_type=F32)
         att_ref[c] = values[512:520] + values[520:528] + values[528:536]
@@ -481,15 +508,13 @@
     shade.start()
     shades.start()
     for c in range(4):
-
-        def finish(at):
-            home(c, at, at).wait_recv()
-            size(c, at, at).wait_recv()
-            out(c, at, at).wait_send()
-            home(c, at, at).wait_send()
-            size(c, at, at).wait_send()
-
-        each(finish)
+        home(c, others, others).wait_recv()
+        size(c, others, others).wait_recv()
+        last(c, others, others).wait_send()
+        if c < 3:
+            out(c, others, others).wait_send()
+        home(c, others, others).wait_send()
+        size(c, others, others).wait_send()
     shade.wait_recv()
     shade.wait_send()
     edges.wait_send()
@@ -501,9 +526,9 @@
     shades.wait()
 
 
-GATHERED = 7
-LOADED = 10
-ARRIVALS = 9
+GATHERED = 10
+LOADED = 11
+ARRIVALS = 11
 FLOWS = 6
 
 
@@ -512,19 +537,19 @@
     gathered, scratch = scratch[:GATHERED], scratch[GATHERED:]
     loaded, scratch = scratch[: LOADED + ARRIVALS], scratch[LOADED + ARRIVALS :]
     flows, scratch = scratch[:FLOWS], scratch[FLOWS:]
-    temporary, scratch = scratch[:5], scratch[5:]
+    temporary, scratch = scratch[:6], scratch[6:]
     held, scratch = scratch[:3], scratch[3:]
     param_sems, out_sems, adv_ref, att_ref, oc_ref = scratch[:5]
     loads = [pltpu.make_async_copy(src, dst, param_sems.at[i]) for i, (src, dst) in enumerate(zip(params, held))]
     for load in loads:
         load.start()
     gather_kernel(nz, nx, *fields, *gathered, *loaded)
-    flow_kernel(*gathered[:6], *flows, *temporary)
+    flow_kernel(*gathered[:9], *flows, *temporary)
     for load in loads:
         load.wait()
     adv_out, back_ref, scale_ref, att_out, attp_ref, oc_out = outs
     react_kernel(
-        nz, *flows, gathered[6], *held, adv_ref, back_ref, scale_ref, att_ref, attp_ref, oc_ref,
+        nz, *flows, gathered[9], *held, adv_ref, back_ref, scale_ref, att_ref, attp_ref, oc_ref,
         adv_out, att_out, oc_out, out_sems, *scratch[5:]
     )
 
@@ -622,23 +647,26 @@
         ),
         in_specs=[pl.BlockSpec(memory_space=pltpu.HBM)] * 9,
         out_specs=(pl.BlockSpec(memory_space=pltpu.HBM),) * 6,
-        scratch_shapes=[pltpu.VMEM((nz, 8, lanes), F32) for lanes in (SPEEDS, WATER, 512, 640, 512, 640)]
+        scratch_shapes=[pltpu.VMEM((nz, 8, lanes), F32) for lanes in (SPEEDS, DENSITY, WATER, 512, 384, 512, 512, 384, 512)]
         + [pltpu.VMEM((4, 16, 80, 128), F32)]
         + [tile] * 4
         + [
             pltpu.VMEM((8, 8, 64), jnp.int32),
             pltpu.VMEM((4, 512, 128), F32),
             pltpu.VMEM((8, SPEEDS), F32),
+            pltpu.VMEM((8, DENSITY), F32),
             pltpu.VMEM((8, WATER), F32),
             pltpu.VMEM((8, 128), F32),
             pltpu.VMEM((8, 128), F32),
             dma((6,)),
-            dma((2, 2, nz)),
+            dma((2,)),
+            dma((2, nz)),
         ]
-        + [dma((2, nz))] * 5
+        + [dma((2,))] * 4
         + [dma((6,))] * 2
+        + [dma((4,))] * 2
         + [row] * 5
-        + [edge, row, row, row, column, column]
+        + [edge, row, row, row, row, column, column]
         + [
             pltpu.VMEM((64, 64), BF16),
             pltpu.VMEM((1, 64), jnp.int32),
@@ -665,9 +693,9 @@
             pltpu.VMEM((4, 4, nz, 8, 128), I16),
             pltpu.VMEM((4, nz, 1, 128), F32),
         ]
-        + [dma((4, nz))] * 4
+        + [dma((4,))] * 4
         + [dma((2,))] * 2
-        + [dma((4, nz))] * 2,
+        + [dma((4,))] * 4,
         compiler_params=pltpu.CompilerParams(collective_id=0, has_side_effects=True, vmem_limit_bytes=60 << 20),
         name="step",
     )(

time: 118 us -> 104 us (0.88)
  Pallas kernels: 116 us -> 102 us
    pallas_call x1, Pallas kernels: 113 us -> 99.8 us  [shards(): pl.pallas_call(functools.partial(step_kernel, nz, nx), out_shape=(sds((4,...]
where the time goes in v4:
time: 104 us; the launch traced here: 103 us
  Pallas kernels  102 us (98%)
    pallas_call x1, Pallas kernels, shards(): pl.pallas_call(functools.partial(step_kernel, nz, nx), out_shape=(sds((4,...  99.8 us
    pallas_call x1, Pallas kernels, shards(): pl.pallas_call(final_kernel, out_shape=(sds((8, 8, 64)),) * 4 + (sds((4,...  2.66 us

profile of v4, /device:TPU:1, one launch (start us, length us, event | category | flops | bytes accessed | tf_op | source)
XLA Modules:
  0.0 103.1 jit_solution(16555181458431610132)
XLA Ops:
  0.6 99.8 %step.1 = (f32[4,4,128,128]{3,2,1,0:T(8,128)}, s16[4,4,16,8,128]{4,3,2,1,0:T(8,128)(2,1)}, f32[4,16,1,128]{3,2,1,0:T(1,128)}, f32[4,8,128]{2,1,0:T(8,128)}, f32[4,8,128]{2,1,0:T(8,128)}, /*index=5*/f32[4,8,512]{2,1,0:T(8,128)}) custom-call(f32[8,8,64]{2,1,0:T(8,128)} %bitcast.16, f32[8,8,64]{2,1,0:T(8,128)} %bitcast.17, f32[8,8,64]{2,1,0:T(8,128)} %bitcast.18, ...), custom_call_target="tpu_custom_call" | custom-call | tf_op jit(solution)/shard_map/step/pallas_call | solution.py:638
  100.4 2.7 %final.1 = (f32[8,8,64]{2,1,0:T(8,128)}, f32[8,8,64]{2,1,0:T(8,128)}, f32[8,8,64]{2,1,0:T(8,128)}, f32[8,8,64]{2,1,0:T(8,128)}, f32[4,512,128]{2,1,0:T(8,128)}) custom-call(f32[4,4,128,128]{3,2,1,0:T(8,128)} %get-tuple-element.16.adv_hbm, s16[4,4,16,8,128]{4,3,2,1,0:T(8,128)(2,1)} %get-tuple-element.17.back_hbm, ...), custom_call_target="tpu_custom_call" | custom-call | tf_op jit(solution)/shard_map/final/pallas_call | solution.py:707

commit v5 on v4

--- a/solution.py
+++ b/solution.py
@@ -317,7 +317,7 @@
 
     def last(c, to, at):
         lanes = slice(c * 128, c * 128 + 128)
-        return rdma(send_ref.at[3, to, :, lanes], got.at[3, at, :, lanes], s5.at[c], r5.at[c], to_device(to))
+        return rdma(send_ref.at[2:4, to, :, lanes], got.at[2:4, at, :, lanes], s5.at[c], r5.at[c], to_device(to))
 
     def home(c, to, at):
         return rdma(res.at[c, :, to], back_ref.at[c, :, at], s2.at[c], r2.at[c], to_device(to))
@@ -452,7 +452,7 @@
             adv_ref[t, k] = new
             send_ref[t, :, :, k * 128 : k * 128 + 128] = new.reshape(16, 8, 128).astype(BF16)
 
-        @pl.when(t < 3)
+        @pl.when(t < 2)
         def _():
             each(lambda to: out(t, to, z).start())
 
@@ -488,7 +488,7 @@
             oc_ref[f, :, k * 128 : k * 128 + 128] = tr[pl.ds(mine, 8), :]
     ocean.start()
 
-    for t in range(3):
+    for t in range(2):
         out(t, others, others).wait_recv()
     for c in range(4):
         last(c, others, others).wait_recv()
@@ -511,7 +511,7 @@
         home(c, others, others).wait_recv()
         size(c, others, others).wait_recv()
         last(c, others, others).wait_send()
-        if c < 3:
+        if c < 2:
             out(c, others, others).wait_send()
         home(c, others, others).wait_send()
         size(c, others, others).wait_send()

time: 104 us -> 102 us (0.981)
    pallas_call x1, Pallas kernels: 99.8 us -> 98 us  [shards(): pl.pallas_call(functools.partial(step_kernel, nz, nx), out_shape=(sds((4,...]
where the time goes in v5:
time: 102 us; the launch traced here: 101 us
  Pallas kernels  101 us (99%)
    pallas_call x1, Pallas kernels, shards(): pl.pallas_call(functools.partial(step_kernel, nz, nx), out_shape=(sds((4,...  98 us
    pallas_call x1, Pallas kernels, shards(): pl.pallas_call(final_kernel, out_shape=(sds((8, 8, 64)),) * 4 + (sds((4,...  2.66 us

profile of v5, /device:TPU:1, one launch (start us, length us, event | category | flops | bytes accessed | tf_op | source)
XLA Modules:
  0.0 101.3 jit_solution(11175127097510653528)
XLA Ops:
  0.6 98.0 %step.1 = (f32[4,4,128,128]{3,2,1,0:T(8,128)}, s16[4,4,16,8,128]{4,3,2,1,0:T(8,128)(2,1)}, f32[4,16,1,128]{3,2,1,0:T(1,128)}, f32[4,8,128]{2,1,0:T(8,128)}, f32[4,8,128]{2,1,0:T(8,128)}, /*index=5*/f32[4,8,512]{2,1,0:T(8,128)}) custom-call(f32[8,8,64]{2,1,0:T(8,128)} %bitcast.16, f32[8,8,64]{2,1,0:T(8,128)} %bitcast.17, f32[8,8,64]{2,1,0:T(8,128)} %bitcast.18, ...), custom_call_target="tpu_custom_call" | custom-call | tf_op jit(solution)/shard_map/step/pallas_call | solution.py:638
  98.6 2.7 %final.1 = (f32[8,8,64]{2,1,0:T(8,128)}, f32[8,8,64]{2,1,0:T(8,128)}, f32[8,8,64]{2,1,0:T(8,128)}, f32[8,8,64]{2,1,0:T(8,128)}, f32[4,512,128]{2,1,0:T(8,128)}) custom-call(f32[4,4,128,128]{3,2,1,0:T(8,128)} %get-tuple-element.16.adv_hbm, s16[4,4,16,8,128]{4,3,2,1,0:T(8,128)(2,1)} %get-tuple-element.17.back_hbm, ...), custom_call_target="tpu_custom_call" | custom-call | tf_op jit(solution)/shard_map/final/pallas_call | solution.py:707
